TPU v7x, 32 devices: a whole 2x2x4 slice. The times are simulated.
32 devices in a mesh: seq: 8 (over z, x), tp: 4 (over y, core).
Axes of the slice: x: 2, y: 2, z: 4, core: 2. Of those that a mesh axis runs over, the one named last changes fastest.
Arguments:
- hidden_in: bfloat16 [4, 24, 3072], P(None, None, 'seq'), may hold values from -30 to 30
- attn_gain: bfloat16 [3072], P('seq'), may hold values from 0.5 to 1.5
- w_query: bfloat16 [3072, 3072], P('seq', 'tp'), may hold values from -0.109375 to 0.109375
- w_key: bfloat16 [3072, 3072], P('seq', 'tp'), may hold values from -0.109375 to 0.109375
- w_value: bfloat16 [3072, 3072], P('seq', 'tp'), may hold values from -0.109375 to 0.109375
- w_out: bfloat16 [3072, 3072], P('tp', 'seq'), may hold values from -0.109375 to 0.109375
- mlp_gain: bfloat16 [3072], P('seq'), may hold values from 0.5 to 1.5
- w_gate: bfloat16 [3072, 8192], P('seq', 'tp'), may hold values from -0.109375 to 0.109375
- w_up: bfloat16 [3072, 8192], P('seq', 'tp'), may hold values from -0.109375 to 0.109375
- w_down: bfloat16 [8192, 3072], P('tp', 'seq'), may hold values from -0.0625 to 0.0625
- kv_pages: bfloat16 [2, 1664, 32, 3072], P(None, 'seq', None, 'tp'), may hold values from -260 to 260
- lengths: int32 [24], replicated, may hold values from 512 to 2044, as said below
- group_ids: int32 [24], replicated, may hold values from 0 to 1, as said below
- shared_table: int32 [2, 16], replicated, may hold values from 0 to 207, as said below
- own_table: int32 [24, 64], P(None, 'seq'), may hold values from 0 to 207, as said below
Outputs:
- hidden_out: bfloat16 [4, 24, 3072], P(None, None, 'seq')
- new_cache: bfloat16 [2, 4, 24, 3072], P(None, None, None, 'tp')
Inputs may be any that keep to these rules, and one draw needn't show every extreme that they name: `lengths`: one request in every draw has the length 2044. `group_ids`: each group number is named by exactly 12 requests. Entries are pages of the pool of the index of seq that holds the page's positions (prompt page p lies on index p // 8); on one index the pages named by shared_table and own_table are all different. `own_table`: entries are pages of the pool of the index of seq that holds the page's positions; entries of logical pages under 16 are never read.
All inputs are finite; a program needn't handle non-finite values.
Results may differ from a plain program's by a relative error of at most 0.0085.
The roundings to bfloat16 on the way count: a program that leaves them out, or rounds other values in their place, can miss the bound.
Values may be sent and summed in bfloat16 or wider, within the bound.
A program may use at most 192 MiB of HBM per device.

v0:
```python
import math

import jax
import jax.numpy as jnp
from jax import lax
from jax.sharding import PartitionSpec as P

D = 3072
HEAD_DIM = 96
SINKS = 4
WINDOW = 1024


EPSILON = 1e-05
ROPE_BASE = 10000.0
NEGATIVE = -1e30


def rotate(vector, position):
    halfway = vector.shape[-1] // 2
    frequency = ROPE_BASE ** (-(jnp.arange(halfway, dtype=jnp.float32) * 2.0 / vector.shape[-1]))
    angles = position[..., None].astype(jnp.float32) * frequency
    cosine = jnp.cos(angles)
    sine_part = jnp.sin(angles)
    first_half = vector[..., :halfway]
    second_half = vector[..., halfway:]
    return jnp.concatenate(
        [
            first_half * cosine - second_half * sine_part,
            second_half * cosine + first_half * sine_part,
        ],
        -1,
    )


def seq_total(partial_value, squares):
    return lax.psum((partial_value, squares), "seq")


def head_total(partial_value):
    return lax.psum(partial_value, "tp")


def body(
    hidden_in,
    attn_gain,
    w_query,
    w_key,
    w_value,
    w_out,
    mlp_gain,
    w_gate,
    w_up,
    w_down,
    kv_pages,
    lengths,
    group_ids,
    shared_table,
    own_table,
):
    seq_index = lax.axis_index("seq")
    step_count = hidden_in.shape[0]
    requests = hidden_in.shape[1]
    local_width = hidden_in.shape[2]
    head_cols = w_query.shape[1]
    local_heads = head_cols // HEAD_DIM
    unit_cols = w_gate.shape[1]
    page_rows = kv_pages.shape[2]
    local_pages = own_table.shape[1]
    block_len = local_pages * page_rows
    group_count = shared_table.shape[0]
    prompt_pages = shared_table.shape[1]
    score_scale = 1.0 / math.sqrt(HEAD_DIM)
    flat_rows = step_count * requests
    logical = seq_index * local_pages + jnp.arange(local_pages, dtype=jnp.int32)
    group_pick = (group_ids[:, None] == jnp.arange(group_count, dtype=jnp.int32)[None, :]).astype(
        jnp.int32
    )
    group_rows = jnp.sum(group_pick[:, :, None] * shared_table[None, :, :], axis=1)
    column_pick = (logical[:, None] == jnp.arange(prompt_pages, dtype=jnp.int32)[None, :]).astype(
        jnp.int32
    )
    shared_local = jnp.sum(group_rows[:, None, :] * column_pick[None, :, :], axis=2)
    physical = jnp.where(logical[None, :] < prompt_pages, shared_local, own_table)
    gathered = kv_pages[:, physical]
    cached_keys = gathered[0].reshape(requests, block_len, local_heads, HEAD_DIM)
    cached_values = (
        gathered[1].reshape(requests, block_len, local_heads, HEAD_DIM).astype(jnp.float32)
    )
    positions = seq_index * block_len + jnp.arange(block_len, dtype=jnp.int32)
    step_ids = jnp.arange(step_count, dtype=jnp.int32)
    owner_new = jnp.transpose((lengths[None, :] + step_ids[:, None]) // block_len == seq_index)
    attn_scale = attn_gain.astype(jnp.float32)
    mlp_scale = mlp_gain.astype(jnp.float32)
    w_pair = jnp.concatenate([w_gate, w_up], axis=1)
    residual = hidden_in.astype(jnp.float32).reshape(flat_rows, local_width)
    normed = (residual * attn_scale).astype(jnp.bfloat16)
    squares = jnp.sum(residual * residual, axis=-1)
    where_now = lengths[None, :] + step_ids[:, None]
    w_qkv = jnp.concatenate([w_query, w_key, w_value], axis=1)
    partial_value = jnp.dot(normed, w_qkv, preferred_element_type=jnp.float32)
    summed, square_sum = seq_total(partial_value, squares)
    inv_rms = lax.rsqrt(square_sum / D + EPSILON)
    projected = (summed * inv_rms[:, None]).reshape(step_count, requests, 3, local_heads, HEAD_DIM)
    queries = rotate(projected[:, :, 0], where_now[:, :, None]).astype(jnp.bfloat16)
    key_new = (
        rotate(projected[:, :, 1], where_now[:, :, None])
        .astype(jnp.bfloat16)
        .reshape(step_count, requests, head_cols)
    )
    value_new = projected[:, :, 2].astype(jnp.bfloat16).reshape(step_count, requests, head_cols)
    store_keys = key_new.reshape(step_count, requests, local_heads, HEAD_DIM)
    store_values = value_new.reshape(step_count, requests, local_heads, HEAD_DIM).astype(
        jnp.float32
    )
    in_window = positions[None, None, :] > lengths[None, :, None] + step_ids[:, None, None] - WINDOW
    is_live = (positions[None, None, :] < lengths[None, :, None]) & (
        (positions[None, None, :] < SINKS) | in_window
    )
    new_live = (step_ids[None, None, :] <= step_ids[:, None, None]) & owner_new[None, :, :]
    scores = (
        jnp.einsum("tbhd,bkhd->tbhk", queries, cached_keys, preferred_element_type=jnp.float32)
        * score_scale
    )
    new_scores = (
        jnp.einsum("tbhd,sbhd->tbhs", queries, store_keys, preferred_element_type=jnp.float32)
        * score_scale
    )
    scores = jnp.where(is_live[:, :, None, :], scores, NEGATIVE)
    new_scores = jnp.where(new_live[:, :, None, :], new_scores, NEGATIVE)
    local_peak = jnp.maximum(jnp.max(scores, axis=-1), jnp.max(new_scores, axis=-1))
    score_peak = lax.pmax(local_peak, "seq")
    weights = jnp.where(is_live[:, :, None, :], jnp.exp(scores - score_peak[..., None]), 0.0)
    new_weights = jnp.where(
        new_live[:, :, None, :], jnp.exp(new_scores - score_peak[..., None]), 0.0
    )
    weight_sum = jnp.sum(weights, axis=-1) + jnp.sum(new_weights, axis=-1)
    weighted = jnp.einsum("tbhk,bkhd->tbhd", weights, cached_values) + jnp.einsum(
        "tbhs,sbhd->tbhd", new_weights, store_values
    )
    local_sum = weight_sum
    local_weighted = weighted
    weight_sum, weighted = lax.psum((local_sum, local_weighted), "seq")
    attn = (weighted / weight_sum[..., None]).astype(jnp.bfloat16).reshape(flat_rows, head_cols)
    mid_rows = residual + head_total(jnp.dot(attn, w_out, preferred_element_type=jnp.float32))
    mlp_in = (mid_rows * mlp_scale).astype(jnp.bfloat16)
    mid_squares = jnp.sum(mid_rows * mid_rows, axis=-1)
    gate_up = jnp.dot(mlp_in, w_pair, preferred_element_type=jnp.float32)
    pair_sum, mid_sum = seq_total(gate_up, mid_squares)
    inv_mid = lax.rsqrt(mid_sum / D + EPSILON)[:, None]
    activated = (
        jax.nn.silu(pair_sum[:, :unit_cols] * inv_mid) * (pair_sum[:, unit_cols:] * inv_mid)
    ).astype(jnp.bfloat16)
    result = (
        mid_rows + head_total(jnp.dot(activated, w_down, preferred_element_type=jnp.float32))
    ).astype(jnp.bfloat16)
    hidden_out = result.reshape(step_count, requests, local_width)
    return (hidden_out, jnp.stack([key_new, value_new]))


def solution(mesh):
    return jax.shard_map(
        body,
        mesh=mesh,
        in_specs=(
            P(None, None, "seq"),
            P("seq"),
            P("seq", "tp"),
            P("seq", "tp"),
            P("seq", "tp"),
            P("tp", "seq"),
            P("seq"),
            P("seq", "tp"),
            P("seq", "tp"),
            P("tp", "seq"),
            P(None, "seq", None, "tp"),
            P(),
            P(),
            P(),
            P(None, "seq"),
        ),
        out_specs=(P(None, None, "seq"), P(None, None, None, "tp")),
        check_vma=False,
    )
```

profile of v0, /device:TPU:0, one launch (start us, length us, event | category | flops | bytes accessed | tf_op | source)
XLA Modules:
  0.0 413.2 jit_solution(18278633913271878751)
XLA Ops:
  7.3 0.8 convert_element_type.82
  8.1 0.9 fusion.40
  9.0 2.8 fusion.8
  11.8 0.1 fusion.39
  12.1 0.1 multiply_reduce_fusion.2
  12.2 0.1 multiply_reduce_fusion.1
  12.3 0.1 copy.33
  12.4 0.1 reshape.251
  12.5 16.8 %gather_fusion = bf16[192,2,32,768]{3,2,1,0:T(8,128)(2,1)} fusion(bf16[2,208,32,768]{3,2,1,0:T(8,128)(2,1)} %param.25, s32[1024]{0:T(1024)S(1)} %pad_clamp_fusion), kind=kCustom, calls=%fused_computation | custom fusion | bytes 37749504 | tf_op jit(solution)/shard_map/gather | solution.py:85
  29.3 9.6 %copy.69 = bf16[24,8,2,32,768]{4,3,1,0,2:T(8,128)(2,1)S(1)} copy(bf16[24,8,2,32,768]{4,3,2,1,0:T(8,128)(2,1)} %bitcast.48) | data formatting | bytes 37748736 | tf_op jit(solution)/shard_map/gather | solution.py:85
  38.9 6.9 %fusion.55 = (bf16[1,24,8,32,768]{4,3,2,1,0:T(8,128)(2,1)}, bf16[1,24,8,32,768]{4,3,2,1,0:T(8,128)(2,1)}) fusion(bf16[2,24,8,32,768]{4,3,2,1,0:T(8,128)(2,1)S(1)} %bitcast.47), kind=kLoop, calls=%fused_computation.100 | loop fusion | bytes 37748736 | tf_op jit(solution)/shard_map/slice | solution.py:86
  45.8 21.8 %reshape_squeeze.6 = bf16[24,256,8,96]{3,2,1,0:T(8,128)(2,1)} reshape(bf16[1,24,8,32,768]{4,3,2,1,0:T(8,128)(2,1)} %get-tuple-element.3) | data formatting | bytes 18874368 | tf_op jit(solution)/shard_map/reshape;squeeze | solution.py:88
  67.5 0.1 reduce_sum.59
  67.6 24.1 %psum.57 = f32[96]{0:T(128)S(1)} all-reduce(f32[96]{0:T(128)S(1)} %reduce_sum.59), channel_id=1, replica_groups=mesh['seq'=8,'tp'=4] {'seq'}, use_global_device_ids=true, to_apply=%region_4.5 | all-reduce | flops 96 | bytes 768 | tf_op jit(solution)/shard_map/psum | solution.py:37
  91.8 21.8 %reshape_squeeze.7 = bf16[24,256,8,96]{3,2,1,0:T(8,128)(2,1)} reshape(bf16[1,24,8,32,768]{4,3,2,1,0:T(8,128)(2,1)} %get-tuple-element.2) | data formatting | bytes 18874368 | tf_op jit(solution)/shard_map/reshape;squeeze | solution.py:86
  113.5 0.1 fusion.43
  113.7 0.1 broadcast_and_fusion
  113.9 0.1 or_and_fusion
  114.0 0.4 multiply_cosine_fusion
  114.4 2.3 broadcast_multiply_fusion
  116.7 2.0 reshape.246
  118.8 0.5 copy_bitcast_fusion.1
  119.3 0.4 subtract_convert_fusion
  119.7 0.4 multiply_subtract_fusion
  120.1 0.3 maximum_convert_fusion
  120.4 8.1 %fusion.57 = (f32[4,24,8]{0,2,1:T(8,128)S(1)}, f32[4,24,8,256]{3,0,2,1:T(4,128)S(1)}) fusion(bf16[4,24,8,48]{3,0,2,1:T(4,128)(2,1)S(1)} %get-tuple-element.9, bf16[4,24,8,48]{3,0,2,1:T(4,128)(2,1)S(1)} %get-tuple-element.8, bf16[24,256,8,96]{3,2,1,0:T(8,128)(2,1)} %reshape_squeeze.7, pred[4,24,256]{2,0,1:T(4,128)(4,1)S(1)} %or_and_fusion), kind=kOutput, calls=%fused_computation.102 | convolution fusion | flops 38632704 | bytes 10398720 | tf_op jit(solution)/shard_map/tbhd,bkhd->tbhk/dot_general | solution.py:122
  128.5 1.6 fusion.58
  130.2 33.8 %pmax.7 = f32[4,24,8]{0,2,1:T(8,128)S(1)} all-reduce(f32[4,24,8]{0,2,1:T(8,128)S(1)} %max.5), channel_id=1, replica_groups=mesh['seq'=8,'tp'=4] {'seq'}, use_global_device_ids=true, to_apply=%region_7.8 | all-reduce | flops 768 | bytes 6144 | tf_op jit(solution)/shard_map/pmax | solution.py:132
  164.0 7.2 %fusion = f32[24,8,96,4]{2,3,1,0:T(4,128)} fusion(bf16[24,256,8,96]{3,2,1,0:T(8,128)(2,1)} %reshape_squeeze.6, f32[4,24,8,256]{3,0,2,1:T(4,128)S(1)} %get-tuple-element.17, f32[4,24,8]{0,2,1:T(8,128)S(1)} %pmax.7, pred[4,24,256]{2,0,1:T(4,128)(4,1)S(1)} %or_and_fusion), kind=kOutput, calls=%fused_computation.2 | convolution fusion | flops 38141952 | bytes 10546176 | tf_op jit(solution)/shard_map/tbhk,bkhd->tbhd/dot_general | solution.py:138
  171.1 2.3 fusion.21
  173.5 0.4 fusion.34
  173.9 0.6 fusion.28
  174.5 36.2 %psum.59 = f32[4,24,8]{0,2,1:T(8,128)S(1)} all-reduce(f32[4,24,8]{0,2,1:T(8,128)S(1)} %add.156), channel_id=1, replica_groups=mesh['seq'=8,'tp'=4] {'seq'}, use_global_device_ids=true, to_apply=%region_11.12 | all-reduce | flops 768 | bytes 6144 | tf_op jit(solution)/shard_map/psum | solution.py:143
  210.7 33.2 %all-reduce.8.cloned.1.call-done = f32[4,24,8,96]{3,0,2,1:T(4,128)} async-done(((f32[4,24,8,96]{3,0,2,1:T(4,128)}), f32[4,24,8,96]{3,0,2,1:T(4,128)}) %all-reduce.8.cloned.1.call-update) | async-done | bytes 294928 | tf_op jit(solution)/shard_map/psum | solution.py:143
  243.9 1.3 divide_convert_fusion
  245.2 0.2 reshape.247
  245.4 2.0 fusion.59
  247.5 29.9 %all-reduce.10.cloned.1.call-done = f32[96,384]{1,0:T(8,128)} async-done(((f32[96,384]{1,0:T(8,128)}), f32[96,384]{1,0:T(8,128)}) %all-reduce.10.cloned.1.call-update) | async-done | bytes 147472 | tf_op jit(solution)/shard_map/psum | solution.py:41
  277.4 1.0 multiply_reduce_fusion
  278.4 3.8 fusion.4
  282.2 0.2 convert_element_type.94
  282.5 0.2 convert_element_type.93
  282.6 22.1 %psum.62 = f32[96]{0:T(128)S(1)} all-reduce(f32[96]{0:T(128)S(1)} %get-tuple-element.10), channel_id=1, replica_groups=mesh['seq'=8,'tp'=4] {'seq'}, use_global_device_ids=true, to_apply=%region_15.16 | all-reduce | flops 96 | bytes 768 | tf_op jit(solution)/shard_map/psum | solution.py:37
  304.8 67.5 %all-reduce.12.cloned.1.call-done = f32[96,4096]{1,0:T(8,128)} async-done(((f32[96,4096]{1,0:T(8,128)}), f32[96,4096]{1,0:T(8,128)}) %all-reduce.12.cloned.1.call-update) | async-done | bytes 1572880 | tf_op jit(solution)/shard_map/psum | solution.py:37
  372.3 2.5 fusion.32
  374.8 0.7 pad_maximum_fusion
  375.6 29.5 %all-reduce.14.cloned.1.call-done = f32[96,384]{1,0:T(8,128)} async-done(((f32[96,384]{1,0:T(8,128)}), f32[96,384]{1,0:T(8,128)}) %all-reduce.14.cloned.1.call-update) | async-done | bytes 147472 | tf_op jit(solution)/shard_map/psum | solution.py:41
  405.1 1.6 add_convert_fusion.1
  (52 shorter events, 1.0 us)
Async XLA Ops:
  7.2 365.1 %copy-start = (bf16[2048,384]{1,0:T(8,128)(2,1)S(1)}, bf16[2048,384]{1,0:T(8,128)(2,1)}, u32[]{:S(2)}) copy-start(bf16[2048,384]{1,0:T(8,128)(2,1)} %param.24) | copy-start | bytes 4718596
  7.2 4.7 %copy-start.1 = (bf16[4,24,384]{2,1,0:T(8,128)(2,1)S(1)}, bf16[4,24,384]{2,1,0:T(8,128)(2,1)}, u32[]{:S(2)}) copy-start(bf16[4,24,384]{2,1,0:T(8,128)(2,1)} %param.15) | copy-start | bytes 221188
  7.2 4.9 %copy-start.9 = (s32[24]{0:T(128)S(1)}, s32[24]{0:T(128)}, u32[]{:S(2)}) copy-start(s32[24]{0:T(128)} %param.27) | copy-start | bytes 292
  7.2 4.9 %copy-start.7 = (s32[2,16]{1,0:T(2,128)S(1)}, s32[2,16]{1,0:T(2,128)}, u32[]{:S(2)}) copy-start(s32[2,16]{1,0:T(2,128)} %param.28) | copy-start | bytes 388
  7.2 5.0 %copy-start.6 = (s32[24,8]{0,1:T(8,128)S(1)}, s32[24,8]{0,1:T(8,128)}, u32[]{:S(2)}) copy-start(s32[24,8]{0,1:T(8,128)} %param.29) | copy-start | bytes 2308
  7.2 107.2 %all-reduce.6.cloned.1.call-start = ((), (), s32[]{:S(2)}) async-start(), calls=%async_computation | async-start | bytes 1769472 | tf_op jit(solution)/shard_map/psum | solution.py:37
  11.7 232.2 %all-reduce.8.cloned.1.call-start = ((), (), s32[]{:S(2)}) async-start(), calls=%async_computation.1 | async-start | bytes 786432 | tf_op jit(solution)/shard_map/psum | solution.py:143
  91.8 21.8 %copy-start.5 = (s32[24]{0:T(128)S(1)}, s32[24]{0:T(128)}, u32[]{:S(2)}) copy-start(s32[24]{0:T(128)} %param.26) | copy-start | bytes 292
  119.7 0.7 copy-start.3
  119.7 0.7 copy-start.4
  171.1 76.4 %copy-start.8 = (bf16[384]{0:T(512)(128)(2,1)S(1)}, bf16[384]{0:T(512)(128)(2,1)}, u32[]{:S(2)}) copy-start(bf16[384]{0:T(512)(128)(2,1)} %param.21) | copy-start | bytes 2308
  173.4 104.0 %all-reduce.10.cloned.1.call-start = ((), (), s32[]{:S(2)}) async-start(), calls=%async_computation.2 | async-start | bytes 294912 | tf_op jit(solution)/shard_map/psum | solution.py:41
  247.4 124.9 %all-reduce.12.cloned.1.call-start = ((), (), s32[]{:S(2)}) async-start(), calls=%async_computation.3 | async-start | bytes 3145728 | tf_op jit(solution)/shard_map/psum | solution.py:37
  282.2 122.9 %all-reduce.14.cloned.1.call-start = ((), (), s32[]{:S(2)}) async-start(), calls=%async_computation.4 | async-start | bytes 294912 | tf_op jit(solution)/shard_map/psum | solution.py:41
  282.4 122.7 %copy-start.2 = (f32[96,384]{1,0:T(8,128)S(1)}, f32[96,384]{1,0:T(8,128)}, u32[]{:S(2)}) copy-start(f32[96,384]{1,0:T(8,128)} %all-reduce.10.cloned.1.call-done) | copy-start | bytes 442372
Sparse Core Ops, SparseCore 0:
  11.9 78.9 all-reduce.5
  173.5 70.3 all-reduce.7
  247.5 29.7 all-reduce.9
  282.3 89.9 all-reduce.11
  374.9 30.1 all-reduce.13
where the time goes:
time: 415 us; the launch traced here: 413 us
  waiting for transfers between devices  160 us (39%)
  blocking collectives  116 us (28%)
  local copies, waits for them, and re-layouts  80.3 us (19%)
  matrix products  30.1 us (7%)
  between operations  14.1 us (3%)
  other arithmetic  11.9 us (3%)
    psum x2, waiting for transfers between devices, seq_total(): return lax.psum((partial_value, squares), 'seq')  67.6 us
    psum x2, waiting for transfers between devices, head_total(): return lax.psum(partial_value, 'tp')  59.4 us
    psum x2, blocking collectives, seq_total(): return lax.psum((partial_value, squares), 'seq')  46.3 us
    psum x1, blocking collectives, body(): weight_sum, weighted = lax.psum((local_sum, local_weighted), 'seq')  36.2 us
    pmax x1, blocking collectives, body(): score_peak = lax.pmax(local_peak, 'seq')  33.8 us
    psum x1, waiting for transfers between devices, body(): weight_sum, weighted = lax.psum((local_sum, local_weighted), 'seq')  33.2 us
    gather x2, local copies, waits for them, and re-layouts, body(): gathered = kv_pages[:, physical]  26.4 us
    another operation x1, local copies, waits for them, and re-layouts, body(): gathered[1].reshape(requests, block_len, local_heads, HEAD_DIM)  21.8 us
  transfers between devices with their start and end apart: 5, of which 4 were waited for; matrix products, arithmetic and copies ran while one was open for 19% of the time, Pallas kernels for 0%

commit v1 on v0

--- a/solution.py
+++ b/solution.py
@@ -1,8 +1,11 @@
+import functools
 import math
 
 import jax
 import jax.numpy as jnp
 from jax import lax
+from jax.experimental import pallas as pl
+from jax.experimental.pallas import tpu as pltpu
 from jax.sharding import PartitionSpec as P
 
 D = 3072
@@ -158,9 +161,601 @@
     return (hidden_out, jnp.stack([key_new, value_new]))
 
 
+MESH_ID = pl.DeviceIdType.MESH
+LANES = 128
+HALF_LANES = 64
+
+
+def greet(axes):
+    barrier = pltpu.get_barrier_semaphore()
+    total = 0
+    for axis, size in axes:
+        me = lax.axis_index(axis)
+        for step in range(1, size):
+            pl.semaphore_signal(
+                barrier,
+                inc=1,
+                device_id={axis: lax.rem(me + step, size)},
+                device_id_type=MESH_ID,
+            )
+            total += 1
+    pl.semaphore_wait(barrier, total)
+
+
+def send(source, target, axis, peer, send_sem, recv_sem):
+    copy = pltpu.make_async_remote_copy(
+        src_ref=source,
+        dst_ref=target,
+        send_sem=send_sem,
+        recv_sem=recv_sem,
+        device_id={axis: peer},
+        device_id_type=MESH_ID,
+    )
+    copy.start()
+    return copy
+
+
+def project_kernel(
+    n,
+    x_ref,
+    gain_ref,
+    wq_ref,
+    wk_ref,
+    wv_ref,
+    cos_ref,
+    sin_ref,
+    out_ref,
+    partial,
+    chunks,
+    landed,
+    shared,
+    send_a,
+    recv_a,
+    send_b,
+    recv_b,
+):
+    me = lax.axis_index("seq")
+    rows = chunks.shape[1]
+    cols = wq_ref.shape[1]
+    width = 3 * cols
+    steps = out_ref.shape[1]
+    x = x_ref[...].astype(jnp.float32)
+    normed = (x * gain_ref[...].astype(jnp.float32)).astype(jnp.bfloat16)
+    squares = jnp.sum(x * x, axis=-1, keepdims=True)
+    for index, weight in enumerate((wq_ref, wk_ref, wv_ref)):
+        partial[:, index * cols : (index + 1) * cols] = jnp.dot(
+            normed, weight[...], preferred_element_type=jnp.float32
+        )
+    partial[:, width:] = jnp.broadcast_to(squares, (x.shape[0], LANES))
+    for j in range(n):
+        chunks[j] = partial[j * rows : (j + 1) * rows, :]
+    greet((("seq", n),))
+    copies = []
+    for d in range(1, n):
+        peer = lax.rem(me + d, n)
+        copies.append(
+            send(chunks.at[peer], landed.at[d - 1], "seq", peer, send_a.at[d - 1], recv_a.at[d - 1])
+        )
+    total = chunks[me]
+    for d in range(1, n):
+        copies[d - 1].wait_recv()
+        total = total + landed[d - 1]
+    inv_rms = lax.rsqrt(total[:, width : width + 1] / D + EPSILON)
+    projected = total[:, :width] * inv_rms
+    lane = lax.broadcasted_iota(jnp.int32, (rows, cols), 1)
+    early = lax.rem(lane, HEAD_DIM) < HEAD_DIM // 2
+    cosine = cos_ref[me]
+    sine = sin_ref[me]
+
+    def turn(vector):
+        ahead = pltpu.roll(vector, cols - HEAD_DIM // 2, 1)
+        behind = pltpu.roll(vector, HEAD_DIM // 2, 1)
+        return vector * cosine + jnp.where(early, -ahead, behind) * sine
+
+    ready = jnp.concatenate(
+        [
+            turn(projected[:, :cols]),
+            turn(projected[:, cols : 2 * cols]),
+            projected[:, 2 * cols :],
+        ],
+        axis=1,
+    ).astype(jnp.bfloat16)
+    shared[me, 0:rows] = ready
+    outgoing = []
+    for d in range(1, n):
+        peer = lax.rem(me + d, n)
+        outgoing.append(
+            send(shared.at[me], shared.at[me], "seq", peer, send_b.at[d - 1], recv_b.at[d - 1])
+        )
+    for copy in copies:
+        copy.wait_send()
+    for copy in outgoing:
+        copy.wait_recv()
+    for j in range(n):
+        held = shared[j].astype(jnp.float32)
+        for i in range(rows // steps):
+            out_ref[j * (rows // steps) + i] = held[i * steps : (i + 1) * steps]
+    for copy in outgoing:
+        copy.wait_send()
+
+
+def attend_kernel(
+    lengths_ref, pages_ref, qkv_ref, kv_ref, out_ref, pages, page_sem
+):
+    seq_index = lax.axis_index("seq")
+    requests, steps = qkv_ref.shape[0], qkv_ref.shape[1]
+    cols = pages.shape[-1]
+    block_len = pages.shape[2]
+    local_pages = page_sem.shape[1]
+    page_rows = block_len // local_pages
+    heads = cols // HEAD_DIM
+    base = seq_index * block_len
+    scale = 1.0 / math.sqrt(HEAD_DIM)
+
+    def page_copy(b, p):
+        return pltpu.make_async_copy(
+            kv_ref.at[:, pages_ref[b, p]],
+            pages.at[b, :, pl.ds(p * page_rows, page_rows)],
+            page_sem.at[b, p],
+        )
+
+    def is_used(b):
+        length = lengths_ref[b]
+        return (base < length + steps) & ((base < SINKS) | (base + block_len > length - WINDOW))
+
+    @pl.loop(0, requests)
+    def _(b):
+        @pl.when(is_used(b))
+        def _():
+            for p in range(local_pages):
+                page_copy(b, p).start()
+
+    head_row = lax.broadcasted_iota(jnp.int32, (heads, cols), 0) * HEAD_DIM
+    head_lane = lax.broadcasted_iota(jnp.int32, (heads, cols), 1)
+    own = jnp.where((head_lane >= head_row) & (head_lane < head_row + HEAD_DIM), 1.0, 0.0)
+    stat_lane = lax.broadcasted_iota(jnp.int32, (heads, LANES), 1)
+    stat_row = lax.broadcasted_iota(jnp.int32, (heads, LANES), 0)
+    pick_peak = jnp.where(stat_lane == stat_row, 1.0, 0.0)
+    pick_sum = jnp.where(stat_lane == stat_row + HALF_LANES, 1.0, 0.0)
+    row_step = lax.broadcasted_iota(jnp.int32, (steps * heads, block_len), 0) // heads
+    place = base + lax.broadcasted_iota(jnp.int32, (steps * heads, block_len), 1)
+    page_row = lax.broadcasted_iota(jnp.int32, (page_rows, cols), 0)
+    idle_lane = lax.broadcasted_iota(jnp.int32, (steps, cols + LANES), 1)
+    idle = jnp.where((idle_lane >= cols) & (idle_lane < cols + HALF_LANES), NEGATIVE, 0.0)
+
+    @pl.loop(0, requests)
+    def _(b):
+        used = is_used(b)
+
+        @pl.when(jnp.logical_not(used))
+        def _():
+            out_ref[b] = idle
+
+        @pl.when(used)
+        def _():
+            length = lengths_ref[b]
+            for p in range(local_pages):
+                page_copy(b, p).wait()
+            for u in range(steps):
+                spot = length + u - base
+
+                @pl.when((spot >= 0) & (spot < block_len))
+                def _():
+                    top = pl.multiple_of(spot // page_rows * page_rows, page_rows)
+                    hit = page_row == spot - top
+                    for kind in range(2):
+                        fresh = qkv_ref[b, u : u + 1, (kind + 1) * cols : (kind + 2) * cols]
+                        old = pages[b, kind, pl.ds(top, page_rows), :].astype(jnp.float32)
+                        pages[b, kind, pl.ds(top, page_rows), :] = jnp.where(
+                            hit, fresh, old
+                        ).astype(jnp.bfloat16)
+
+            wide = jnp.concatenate(
+                [qkv_ref[b, t : t + 1, :cols] * own for t in range(steps)], axis=0
+            ).astype(jnp.bfloat16)
+            scores = (
+                lax.dot_general(
+                    wide,
+                    pages[b, 0],
+                    (((1,), (1,)), ((), ())),
+                    preferred_element_type=jnp.float32,
+                )
+                * scale
+            )
+            reach = length + row_step
+            live = (place <= reach) & ((place < SINKS) | (place > reach - WINDOW))
+            scores = jnp.where(live, scores, NEGATIVE)
+            peak = jnp.max(scores, axis=-1, keepdims=True)
+            weights = jnp.where(live, jnp.exp(scores - peak), 0.0)
+            weight_sum = jnp.sum(weights, axis=-1, keepdims=True)
+            coarse = weights.astype(jnp.bfloat16)
+            fine = (weights - coarse.astype(jnp.float32)).astype(jnp.bfloat16)
+            both = jnp.dot(
+                jnp.concatenate([coarse, fine], axis=0),
+                pages[b, 1],
+                preferred_element_type=jnp.float32,
+            )
+            weighted = both[: steps * heads] + both[steps * heads :]
+            for t in range(steps):
+                part = slice(t * heads, (t + 1) * heads)
+                out_ref[b, t : t + 1, :cols] = jnp.sum(weighted[part] * own, axis=0, keepdims=True)
+                out_ref[b, t : t + 1, cols:] = jnp.sum(
+                    peak[part] * pick_peak + weight_sum[part] * pick_sum, axis=0, keepdims=True
+                )
+
+
+def finish_kernel(
+    n,
+    m,
+    att_ref,
+    x_ref,
+    gain_ref,
+    wo_ref,
+    wg_ref,
+    wu_ref,
+    wd_ref,
+    out_ref,
+    chunks,
+    landed,
+    shared,
+    flat,
+    mid_landed,
+    mid_all,
+    pair_out,
+    pair_landed,
+    square_out,
+    square_landed,
+    acts,
+    down_landed,
+    last,
+    send_a,
+    recv_a,
+    send_b,
+    recv_b,
+    send_c,
+    recv_c,
+    send_d,
+    recv_d,
+    send_e,
+    recv_e,
+    send_s,
+    recv_s,
+    send_f,
+    recv_f,
+    send_g,
+    recv_g,
+    send_h,
+    recv_h,
+):
+    me = lax.axis_index("seq")
+    rank = lax.axis_index("tp")
+    rows = chunks.shape[1]
+    steps = att_ref.shape[1]
+    cols = wo_ref.shape[0]
+    group = mid_all.shape[1]
+    flat_rows = flat.shape[0]
+    local_width = flat.shape[1]
+    units = acts.shape[2]
+    per = rows // steps
+    for j in range(n):
+        for i in range(per):
+            chunks[j, i * steps : (i + 1) * steps] = att_ref[j * per + i]
+    greet((("seq", n), ("tp", m)))
+    copies = []
+    for d in range(1, n):
+        peer = lax.rem(me + d, n)
+        copies.append(
+            send(chunks.at[peer], landed.at[d - 1], "seq", peer, send_a.at[d - 1], recv_a.at[d - 1])
+        )
+    for copy in copies:
+        copy.wait_recv()
+    arrived = [chunks[me]] + [landed[d - 1] for d in range(1, n)]
+    stats = [value[:, cols:] for value in arrived]
+    lane = lax.broadcasted_iota(jnp.int32, (rows, LANES), 1)
+    is_peak = lane < HALF_LANES
+    peaks = [jnp.where(is_peak, value, 0.0) for value in stats]
+    top = functools.reduce(jnp.maximum, peaks)
+    factors = [jnp.exp(value - top) for value in peaks]
+    sums = [pltpu.roll(value, HALF_LANES, 1) for value in stats]
+    total_sum = functools.reduce(lambda a, b: a + b, [f * s for f, s in zip(factors, sums)])
+    heads = cols // HEAD_DIM
+    inverse = 1.0 / jnp.where(lane < heads, total_sum, 1.0)
+    spread_row = lax.broadcasted_iota(jnp.int32, (LANES, cols), 0) * HEAD_DIM
+    spread_lane = lax.broadcasted_iota(jnp.int32, (LANES, cols), 1)
+    spread = jnp.where(
+        (spread_lane >= spread_row) & (spread_lane < spread_row + HEAD_DIM), 1.0, 0.0
+    )
+    attn = jnp.zeros((rows, cols), jnp.float32)
+    for factor, value in zip(factors, arrived):
+        share = jnp.where(lane < heads, factor * inverse, 0.0)
+        attn = attn + value[:, :cols] * jnp.dot(
+            share, spread, precision=lax.Precision.HIGHEST, preferred_element_type=jnp.float32
+        )
+    shared[me, 0:rows] = attn.astype(jnp.bfloat16)
+    outgoing = []
+    for d in range(1, n):
+        peer = lax.rem(me + d, n)
+        outgoing.append(
+            send(shared.at[me], shared.at[me], "seq", peer, send_b.at[d - 1], recv_b.at[d - 1])
+        )
+    for copy in copies:
+        copy.wait_send()
+    for copy in outgoing:
+        copy.wait_recv()
+    padded = shared.shape[1]
+    product = jnp.dot(
+        shared[...].reshape(n * padded, cols), wo_ref[...], preferred_element_type=jnp.float32
+    )
+    for j in range(n):
+        flat[j * rows : (j + 1) * rows, :] = product[j * padded : j * padded + rows]
+    for copy in outgoing:
+        copy.wait_send()
+
+    def tp_scatter(target, send_sem, recv_sem):
+        started = []
+        for d in range(1, m):
+            peer = lax.rem(rank + d, m)
+            first = pl.multiple_of(peer * group, group)
+            started.append(
+                send(
+                    flat.at[pl.ds(first, group)],
+                    target.at[d - 1],
+                    "tp",
+                    peer,
+                    send_sem.at[d - 1],
+                    recv_sem.at[d - 1],
+                )
+            )
+        total = flat[pl.ds(pl.multiple_of(rank * group, group), group), :]
+        for d in range(1, m):
+            started[d - 1].wait_recv()
+            total = total + target[d - 1]
+        for copy in started:
+            copy.wait_send()
+        return total
+
+    def tp_gather(buffer, send_sem, recv_sem):
+        started = []
+        for d in range(1, m):
+            peer = lax.rem(rank + d, m)
+            started.append(
+                send(
+                    buffer.at[rank],
+                    buffer.at[rank],
+                    "tp",
+                    peer,
+                    send_sem.at[d - 1],
+                    recv_sem.at[d - 1],
+                )
+            )
+        for copy in started:
+            copy.wait()
+
+    own_rows = pl.ds(pl.multiple_of(rank * group, group), group)
+    mid_own = x_ref[own_rows, :] + tp_scatter(mid_landed, send_c, recv_c)
+    mid_all[rank] = mid_own
+    tp_gather(mid_all, send_d, recv_d)
+    mid = mid_all[...].reshape(flat_rows, local_width)
+    mlp_in = (mid * gain_ref[...].astype(jnp.float32)).astype(jnp.bfloat16)
+    square_out[...] = lax.dot_general(
+        jnp.ones((8, local_width), jnp.float32),
+        mid * mid,
+        (((1,), (1,)), ((), ())),
+        precision=lax.Precision.HIGHEST,
+        preferred_element_type=jnp.float32,
+    )
+    squares = []
+    for d in range(1, n):
+        peer = lax.rem(me + d, n)
+        squares.append(
+            send(square_out, square_landed.at[d - 1], "seq", peer, send_s.at[d - 1], recv_s.at[d - 1])
+        )
+
+    def pair(index):
+        span = pl.ds(pl.multiple_of(index * units, units), units)
+        gate = jnp.dot(mlp_in, wg_ref[:, span], preferred_element_type=jnp.float32)
+        upward = jnp.dot(mlp_in, wu_ref[:, span], preferred_element_type=jnp.float32)
+        return gate, upward
+
+    pairs = []
+    for d in range(1, n):
+        peer = lax.rem(me + d, n)
+        gate, upward = pair(peer)
+        pair_out[d - 1, :, :units] = gate
+        pair_out[d - 1, :, units:] = upward
+        pairs.append(
+            send(
+                pair_out.at[d - 1],
+                pair_landed.at[d - 1],
+                "seq",
+                peer,
+                send_e.at[d - 1],
+                recv_e.at[d - 1],
+            )
+        )
+    gate, upward = pair(me)
+    for copy in squares:
+        copy.wait()
+    square_sum = square_out[...]
+    for d in range(1, n):
+        square_sum = square_sum + square_landed[d - 1]
+    column = lax.dot_general(
+        square_sum,
+        jnp.full((8, units), 0.125, jnp.float32),
+        (((0,), (0,)), ((), ())),
+        precision=lax.Precision.HIGHEST,
+        preferred_element_type=jnp.float32,
+    )
+    inv_mid = lax.rsqrt(column / D + EPSILON)
+    for d in range(1, n):
+        pairs[d - 1].wait_recv()
+        gate = gate + pair_landed[d - 1, :, :units]
+        upward = upward + pair_landed[d - 1, :, units:]
+    gate = gate * inv_mid
+    act = (gate / (1.0 + jnp.exp(-gate)) * (upward * inv_mid)).astype(jnp.bfloat16)
+    acts[0] = act
+    activated = []
+    for d in range(1, n):
+        peer = lax.rem(me + d, n)
+        activated.append(
+            send(acts.at[0], acts.at[d], "seq", peer, send_f.at[d - 1], recv_f.at[d - 1])
+        )
+
+    def down(slot, index):
+        span = pl.ds(pl.multiple_of(index * units, units), units)
+        return jnp.dot(acts[slot], wd_ref[span, :], preferred_element_type=jnp.float32)
+
+    product = down(0, me)
+    for copy in pairs:
+        copy.wait_send()
+    for d in range(1, n):
+        activated[d - 1].wait_recv()
+        product = product + down(d, lax.rem(me + n - d, n))
+    flat[...] = product
+    for copy in activated:
+        copy.wait_send()
+    last[rank] = (mid_own + tp_scatter(down_landed, send_g, recv_g)).astype(jnp.bfloat16)
+    tp_gather(last, send_h, recv_h)
+    out_ref[...] = last[...]
+
+
+def fused_body(
+    n,
+    m,
+    hidden_in,
+    attn_gain,
+    w_query,
+    w_key,
+    w_value,
+    w_out,
+    mlp_gain,
+    w_gate,
+    w_up,
+    w_down,
+    kv_pages,
+    lengths,
+    group_ids,
+    shared_table,
+    own_table,
+):
+    seq_index = lax.axis_index("seq")
+    steps, requests, local_width = hidden_in.shape
+    cols = w_query.shape[1]
+    flat_rows = steps * requests
+    rows = flat_rows // n
+    padded = -(-rows // 16) * 16
+    group = flat_rows // m
+    units = w_gate.shape[1] // n
+    page_rows = kv_pages.shape[2]
+    local_pages = own_table.shape[1]
+    block_len = local_pages * page_rows
+    group_count, prompt_pages = shared_table.shape
+    f32, bf16 = jnp.float32, jnp.bfloat16
+
+    logical = seq_index * local_pages + jnp.arange(local_pages, dtype=jnp.int32)
+    group_pick = (group_ids[:, None] == jnp.arange(group_count, dtype=jnp.int32)[None, :]).astype(
+        jnp.int32
+    )
+    group_rows = jnp.sum(group_pick[:, :, None] * shared_table[None, :, :], axis=1)
+    column_pick = (logical[:, None] == jnp.arange(prompt_pages, dtype=jnp.int32)[None, :]).astype(
+        jnp.int32
+    )
+    shared_local = jnp.sum(group_rows[:, None, :] * column_pick[None, :, :], axis=2)
+    physical = jnp.where(logical[None, :] < prompt_pages, shared_local, own_table)
+
+    x = jnp.transpose(hidden_in, (1, 0, 2)).reshape(flat_rows, local_width)
+    halfway = HEAD_DIM // 2
+    frequency = ROPE_BASE ** (-(jnp.arange(halfway, dtype=f32) * 2.0 / HEAD_DIM))
+    where_now = (lengths[:, None] + jnp.arange(steps, dtype=jnp.int32)[None, :]).reshape(-1)
+    angles = where_now[:, None].astype(f32) * frequency
+    cosine = jnp.tile(jnp.cos(angles), (1, cols // halfway)).reshape(n, rows, cols)
+    sine = jnp.tile(jnp.sin(angles), (1, cols // halfway)).reshape(n, rows, cols)
+
+    vmem = pl.BlockSpec(memory_space=pltpu.VMEM)
+    smem = pl.BlockSpec(memory_space=pltpu.SMEM)
+    dma = pltpu.SemaphoreType.DMA
+    wide = 3 * cols
+    qkv = pl.pallas_call(
+        functools.partial(project_kernel, n),
+        out_shape=jax.ShapeDtypeStruct((requests, steps, wide), f32),
+        in_specs=[vmem] * 7,
+        out_specs=vmem,
+        scratch_shapes=[
+            pltpu.VMEM((flat_rows, wide + LANES), f32),
+            pltpu.VMEM((n, rows, wide + LANES), f32),
+            pltpu.VMEM((n - 1, rows, wide + LANES), f32),
+            pltpu.VMEM((n, padded, wide), bf16),
+        ]
+        + [dma((n - 1,))] * 4,
+        compiler_params=pltpu.CompilerParams(
+            collective_id=0, has_side_effects=True, vmem_limit_bytes=48 << 20
+        ),
+    )(x, attn_gain.reshape(1, -1), w_query, w_key, w_value, cosine, sine)
+    new_cache = jnp.transpose(
+        qkv[:, :, cols:].astype(bf16).reshape(requests, steps, 2, cols), (2, 1, 0, 3)
+    )
+
+    attended = pl.pallas_call(
+        attend_kernel,
+        out_shape=jax.ShapeDtypeStruct((requests, steps, cols + LANES), f32),
+        in_specs=[smem, smem, vmem, pl.BlockSpec(memory_space=pl.ANY)],
+        out_specs=vmem,
+        scratch_shapes=[
+            pltpu.VMEM((requests, 2, block_len, cols), bf16),
+            dma((requests, local_pages)),
+        ],
+        compiler_params=pltpu.CompilerParams(vmem_limit_bytes=48 << 20),
+    )(lengths, physical, qkv, kv_pages)
+
+    result = pl.pallas_call(
+        functools.partial(finish_kernel, n, m),
+        out_shape=jax.ShapeDtypeStruct((m, group, local_width), bf16),
+        in_specs=[vmem] * 7,
+        out_specs=vmem,
+        scratch_shapes=[
+            pltpu.VMEM((n, rows, cols + LANES), f32),
+            pltpu.VMEM((n - 1, rows, cols + LANES), f32),
+            pltpu.VMEM((n, padded, cols), bf16),
+            pltpu.VMEM((flat_rows, local_width), f32),
+            pltpu.VMEM((m - 1, group, local_width), f32),
+            pltpu.VMEM((m, group, local_width), f32),
+            pltpu.VMEM((n - 1, flat_rows, 2 * units), f32),
+            pltpu.VMEM((n - 1, flat_rows, 2 * units), f32),
+            pltpu.VMEM((8, flat_rows), f32),
+            pltpu.VMEM((n - 1, 8, flat_rows), f32),
+            pltpu.VMEM((n, flat_rows, units), bf16),
+            pltpu.VMEM((m - 1, group, local_width), f32),
+            pltpu.VMEM((m, group, local_width), bf16),
+        ]
+        + [dma((n - 1,))] * 4
+        + [dma((m - 1,))] * 4
+        + [dma((n - 1,))] * 6
+        + [dma((m - 1,))] * 4,
+        compiler_params=pltpu.CompilerParams(
+            collective_id=1, has_side_effects=True, vmem_limit_bytes=48 << 20
+        ),
+    )(attended, x.astype(f32), mlp_gain.reshape(1, -1), w_out, w_gate, w_up, w_down)
+    hidden_out = jnp.transpose(result.reshape(requests, steps, local_width), (1, 0, 2))
+    return (hidden_out, new_cache)
+
+
+def fits(n, m):
+    flat_rows = 96
+    return (
+        n > 1
+        and m > 1
+        and flat_rows % (n * 4) == 0
+        and flat_rows % (m * 8) == 0
+        and D // m % LANES == 0
+        and D // m // HEAD_DIM <= 8
+    )
+
+
 def solution(mesh):
+    n, m = mesh.shape["seq"], mesh.shape["tp"]
+    chosen = functools.partial(fused_body, n, m) if fits(n, m) else body
     return jax.shard_map(
-        body,
+        chosen,
         mesh=mesh,
         in_specs=(
             P(None, None, "seq"),

time: 415 us -> 156 us (0.38)
  waiting for transfers between devices: 160 us -> 0 us
  Pallas kernels: 0 us -> 148 us
  blocking collectives: 116 us -> 0 us
  local copies, waits for them, and re-layouts: 80.3 us -> 3.4 us
  matrix products: 30.1 us -> 0 us
  between operations: 14.1 us -> 0.89 us
  other arithmetic: 11.9 us -> 1.27 us
    psum x5 -> x0, waiting for transfers between devices: 160 us -> none  [the longest x2 67.6 us: seq_total(): return lax.psum((partial_value, squares), 'seq')]
    pallas_call x0 -> x3, Pallas kernels: none -> 148 us  [the longest x1 80.5 us: fused_body(): pl.pallas_call(functools.partial(finish_kernel, n, m), out_shape=jax.Shap...]
    psum x3 -> x0, blocking collectives: 82.5 us -> none  [the longest x2 46.3 us: seq_total(): return lax.psum((partial_value, squares), 'seq')]
    another operation x2 -> x4, local copies, waits for them, and re-layouts: 43.5 us -> 0.83 us  [the longest x2 0.42 us: fused_body(): jnp.tile(jnp.cos(angles), (1, cols // halfway)).reshape(n, rows, cols)]
    pmax x1 -> x0, blocking collectives: 33.8 us -> none  [body(): score_peak = lax.pmax(local_peak, 'seq')]
    dot_general x8 -> x0, matrix products: 30.1 us -> none  [the longest x1 8.08 us: body(): jnp.einsum('tbhd,bkhd->tbhk', queries, cached_keys, preferred_element_typ...]
    gather x2 -> x0, local copies, waits for them, and re-layouts: 26.4 us -> none  [body(): gathered = kv_pages[:, physical]]
    slice x3 -> x1, local copies, waits for them, and re-layouts: 6.95 us -> 0.1 us  [fused_body(): qkv[:, :, cols:].astype(bf16).reshape(requests, steps, 2, cols)]
  transfers between devices with their start and end apart: 5 -> 0, of which waited for: 4 -> 0; matrix products, arithmetic and copies ran while one was open for 19% -> 0% of each run, Pallas kernels for 0% -> 0%
where the time goes in v1:
time: 156 us; the launch traced here: 153 us
  Pallas kernels  148 us (95%)
  local copies, waits for them, and re-layouts  3.4 us (2%)
    pallas_call x1, Pallas kernels, fused_body(): pl.pallas_call(functools.partial(finish_kernel, n, m), out_shape=jax.Shap...  80.5 us
    pallas_call x1, Pallas kernels, fused_body(): pl.pallas_call(functools.partial(project_kernel, n), out_shape=jax.ShapeD...  48.6 us
    pallas_call x1, Pallas kernels, fused_body(): pl.pallas_call(attend_kernel, out_shape=jax.ShapeDtypeStruct((requests, s...  18.6 us

profile of v1, /device:TPU:0, one launch (start us, length us, event | category | flops | bytes accessed | tf_op | source)
XLA Modules:
  0.0 153.2 jit_solution(2818085355697914797)
XLA Ops:
  0.6 0.7 add_convert_fusion
  1.4 0.1 convert_element_type.32
  1.5 0.3 multiply_sine_fusion
  1.7 0.1 tile.16
  1.8 0.0 copy-start.8
  1.8 0.0 copy-start.11
  1.8 0.0 copy-start.4
  1.8 0.0 copy-start.5
  1.8 0.0 copy-start.6
  1.9 0.4 tile.17.cos_ref
  2.2 0.1 tile.18
  2.3 0.4 tile.19.sin_ref
  2.6 0.0 copy-done.8
  2.7 0.0 copy-done.11
  2.8 0.2 copy-done.4
  2.9 0.2 copy-done.5
  3.1 0.2 copy-done.6
  3.3 0.0 copy-start.13
  3.3 0.0 copy-start.10
  3.3 0.0 copy-start.9
  3.3 0.0 copy-start.7
  3.3 48.6 %shard_map.158.qkv_ref = f32[24,4,2304]{2,1,0:T(4,128)S(1)} custom-call(bf16[96,384]{1,0:T(8,128)(2,1)S(1)} %reshape.155.x_ref, bf16[1,384]{1,0:T(2,128)(2,1)S(1)} %reshape.156.gain_ref, bf16[384,768]{1,0:T(8,128)(2,1)S(1)} %copy-done.4, bf16[384,768]{1,0:T(8,128)(2,1)S(1)} %copy-done.5, bf16[384,768]{1,0:T(8,128)(2,1)S(1)} %copy-done.6, ...), custom_call_target="tpu_custom_call" | custom-call | tf_op jit(solution)/shard_map/pallas_call | solution.py:678
  51.9 0.1 fusion
  52.0 0.0 copy-done.13
  52.0 0.0 copy-done.10
  52.0 0.1 multiply_reduce_fusion.1
  52.1 0.1 multiply_reduce_fusion
  52.2 0.1 copy.25
  52.3 0.0 copy-done.9
  52.3 0.1 copy.26
  52.3 0.0 copy-done.7
  52.3 0.0 copy-start.12
  52.4 0.0 copy-start
  52.4 0.0 copy-start.1
  52.4 0.0 copy-start.2
  52.4 0.0 copy-start.3
  52.4 18.6 %shard_map.159.att_ref = f32[24,4,896]{2,1,0:T(4,128)S(1)} custom-call(s32[24]{0:T(128)S(1)} %copy-done.7, s32[24,8]{1,0:T(8,128)S(1)} %broadcast_select_fusion.pages_ref, f32[24,4,2304]{2,1,0:T(4,128)S(1)} %shard_map.158.qkv_ref, bf16[2,208,32,768]{3,2,1,0:T(8,128)(2,1)} %kv_ref.1), custom_call_target="tpu_custom_call" | custom-call | tf_op jit(solution)/shard_map/pallas_call | solution.py:698
  71.1 0.0 copy-done.12
  71.1 0.0 copy-done
  71.1 0.0 copy-done.1
  71.1 0.0 copy-done.2
  71.1 0.0 copy-done.3
  71.1 80.5 %shard_map.160 = bf16[4,24,384]{2,1,0:T(8,128)(2,1)S(1)} custom-call(f32[24,4,896]{2,1,0:T(4,128)S(1)} %shard_map.159.att_ref, f32[96,384]{1,0:T(8,128)S(1)} %convert_element_type.33.x_ref, bf16[1,384]{1,0:T(2,128)(2,1)S(1)} %reshape.157.gain_ref, bf16[768,384]{1,0:T(8,128)(2,1)S(1)} %copy-done.3, bf16[384,2048]{1,0:T(8,128)(2,1)S(1)} %copy-done, ...), custom_call_target="tpu_custom_call" | custom-call | tf_op jit(solution)/shard_map/pallas_call | solution.py:710
  151.6 0.6 copy.33
  152.3 0.1 slice.7
  152.4 0.1 reshape.159
  152.5 0.8 copy.32
  (11 shorter events, 0.1 us)
Async XLA Ops:
  1.8 0.9 copy-start.8
  1.8 0.9 copy-start.11
  1.8 1.1 copy-start.4
  1.8 1.3 copy-start.5
  1.8 1.4 copy-start.6
  3.3 48.7 %copy-start.13 = (s32[24]{0:T(128)S(1)}, s32[24]{0:T(128)}, u32[]{:S(2)}) copy-start(s32[24]{0:T(128)} %param.27) | copy-start | bytes 292
  3.3 48.7 %copy-start.10 = (s32[2,16]{1,0:T(2,128)S(1)}, s32[2,16]{1,0:T(2,128)}, u32[]{:S(2)}) copy-start(s32[2,16]{1,0:T(2,128)} %param.28) | copy-start | bytes 388
  3.3 49.0 %copy-start.9 = (s32[24,8]{0,1:T(8,128)S(1)}, s32[24,8]{0,1:T(8,128)}, u32[]{:S(2)}) copy-start(s32[24,8]{0,1:T(8,128)} %param.29) | copy-start | bytes 2308
  3.3 49.1 %copy-start.7 = (s32[24]{0:T(128)S(1)}, s32[24]{0:T(128)}, u32[]{:S(2)}) copy-start(s32[24]{0:T(128)} %lengths_ref.1) | copy-start | bytes 292
  52.3 18.7 %copy-start.12 = (bf16[384]{0:T(512)(128)(2,1)S(1)}, bf16[384]{0:T(512)(128)(2,1)}, u32[]{:S(2)}) copy-start(bf16[384]{0:T(512)(128)(2,1)} %param.21) | copy-start | bytes 2308
  52.4 18.7 %copy-start = (bf16[384,2048]{1,0:T(8,128)(2,1)S(1)}, bf16[384,2048]{1,0:T(8,128)(2,1)}, u32[]{:S(2)}) copy-start(bf16[384,2048]{1,0:T(8,128)(2,1)} %wg_ref.1) | copy-start | bytes 4718596
  52.4 18.7 %copy-start.1 = (bf16[384,2048]{1,0:T(8,128)(2,1)S(1)}, bf16[384,2048]{1,0:T(8,128)(2,1)}, u32[]{:S(2)}) copy-start(bf16[384,2048]{1,0:T(8,128)(2,1)} %wu_ref.1) | copy-start | bytes 4718596
  52.4 18.7 %copy-start.2 = (bf16[2048,384]{1,0:T(8,128)(2,1)S(1)}, bf16[2048,384]{1,0:T(8,128)(2,1)}, u32[]{:S(2)}) copy-start(bf16[2048,384]{1,0:T(8,128)(2,1)} %wd_ref.1) | copy-start | bytes 4718596
  52.4 18.7 %copy-start.3 = (bf16[768,384]{1,0:T(8,128)(2,1)S(1)}, bf16[768,384]{1,0:T(8,128)(2,1)}, u32[]{:S(2)}) copy-start(bf16[768,384]{1,0:T(8,128)(2,1)} %wo_ref.1) | copy-start | bytes 1769476

commit v2 on v1

--- a/solution.py
+++ b/solution.py
@@ -195,6 +195,96 @@
     return copy
 
 
+def place_of(n):
+    me = lax.axis_index("seq")
+    near = lax.rem(me, 2)
+    far = me // 2
+    half = n // 2
+
+    def device(step, other):
+        side = 1 - near if other else near
+        return 2 * lax.rem(far + step + half, half) + side
+
+    return me, half, device
+
+
+def pair_scatter(n, make, put, get, near_out, near_in, far_out, far_in, sems):
+    me, half, device = place_of(n)
+    partner = device(0, True)
+    near_send, near_recv, far_send, far_recv = sems
+    order = list(range(1, half)) + [0]
+    near = {}
+    for d in order:
+        put(near_out, d, make(device(d, True)))
+        near[d] = send(
+            near_out.at[d], near_in.at[d], "seq", partner, near_send.at[d], near_recv.at[d]
+        )
+    far = {}
+    for d in range(1, half):
+        peer = device(d, False)
+        value = make(peer)
+        near[d].wait_recv()
+        put(far_out, d - 1, value + get(near_in, d))
+        far[d] = send(
+            far_out.at[d - 1], far_in.at[d - 1], "seq", peer, far_send.at[d - 1], far_recv.at[d - 1]
+        )
+    total = make(me)
+    near[0].wait_recv()
+    total = total + get(near_in, 0)
+    for d in range(1, half):
+        far[d].wait_recv()
+        total = total + get(far_in, d - 1)
+    return total, list(near.values()) + list(far.values())
+
+
+def pair_gather(n, buffer, sems, arrive):
+    me, half, device = place_of(n)
+    partner = device(0, True)
+    near_send, near_recv, far_send, far_recv = sems
+
+    def share(index, peer, send_sem, recv_sem):
+        return send(buffer.at[index], buffer.at[index], "seq", peer, send_sem, recv_sem)
+
+    far = {}
+    near = {}
+    for d in range(1, half):
+        far[d] = share(me, device(d, False), far_send.at[d - 1], far_recv.at[d - 1])
+    near[0] = share(me, partner, near_send.at[0], near_recv.at[0])
+    arrive(me)
+    for d in range(1, half):
+        far[d].wait_recv()
+        index = device(-d, False)
+        near[d] = share(index, partner, near_send.at[d], near_recv.at[d])
+        arrive(index)
+    for d in range(half):
+        near[d].wait_recv()
+        arrive(device(-d, True))
+    return list(near.values()) + list(far.values())
+
+
+def packed_width(width):
+    return width + -(-width // (2 * LANES)) * LANES
+
+
+def put_rows(ref, slot, value):
+    width = value.shape[1]
+    first = packed_width(width) - width
+    ref[slot, :, :width] = value[:8]
+    ref[slot, 0:4, width:] = value[8:12, :first]
+    ref[slot, 4:8, width : 2 * width - first] = value[8:12, first:]
+    if 2 * first > width:
+        ref[slot, 4:8, 2 * width - first :] = jnp.zeros((4, 2 * first - width), value.dtype)
+
+
+def get_rows(ref, slot, width):
+    first = packed_width(width) - width
+    value = ref[slot]
+    rest = jnp.concatenate(
+        [value[0:4, width:], value[4:8, width : 2 * width - first]], axis=1
+    )
+    return jnp.concatenate([value[:, :width], rest], axis=0)
+
+
 def project_kernel(
     n,
     x_ref,
@@ -206,40 +296,45 @@
     sin_ref,
     out_ref,
     partial,
-    chunks,
-    landed,
+    near_out,
+    near_in,
+    far_out,
+    far_in,
     shared,
-    send_a,
-    recv_a,
-    send_b,
-    recv_b,
+    *sems,
 ):
     me = lax.axis_index("seq")
-    rows = chunks.shape[1]
     cols = wq_ref.shape[1]
     width = 3 * cols
     steps = out_ref.shape[1]
+    rows = cos_ref.shape[1]
     x = x_ref[...].astype(jnp.float32)
     normed = (x * gain_ref[...].astype(jnp.float32)).astype(jnp.bfloat16)
     squares = jnp.sum(x * x, axis=-1, keepdims=True)
+
+    def store(value, first, last):
+        for j in range(n):
+            partial[j, :, first:last] = value[j * rows : (j + 1) * rows]
+
     for index, weight in enumerate((wq_ref, wk_ref, wv_ref)):
-        partial[:, index * cols : (index + 1) * cols] = jnp.dot(
-            normed, weight[...], preferred_element_type=jnp.float32
+        store(
+            jnp.dot(normed, weight[...], preferred_element_type=jnp.float32),
+            index * cols,
+            (index + 1) * cols,
         )
-    partial[:, width:] = jnp.broadcast_to(squares, (x.shape[0], LANES))
-    for j in range(n):
-        chunks[j] = partial[j * rows : (j + 1) * rows, :]
+    store(jnp.broadcast_to(squares, (x.shape[0], LANES)), width, width + LANES)
     greet((("seq", n),))
-    copies = []
-    for d in range(1, n):
-        peer = lax.rem(me + d, n)
-        copies.append(
-            send(chunks.at[peer], landed.at[d - 1], "seq", peer, send_a.at[d - 1], recv_a.at[d - 1])
-        )
-    total = chunks[me]
-    for d in range(1, n):
-        copies[d - 1].wait_recv()
-        total = total + landed[d - 1]
+    total, copies = pair_scatter(
+        n,
+        lambda index: partial[index],
+        put_rows,
+        lambda ref, slot: get_rows(ref, slot, width + LANES),
+        near_out,
+        near_in,
+        far_out,
+        far_in,
+        sems[:4],
+    )
     inv_rms = lax.rsqrt(total[:, width : width + 1] / D + EPSILON)
     projected = total[:, :width] * inv_rms
     lane = lax.broadcasted_iota(jnp.int32, (rows, cols), 1)
@@ -259,23 +354,18 @@
             projected[:, 2 * cols :],
         ],
         axis=1,
+    )
+    shared[me] = jnp.concatenate(
+        [ready, jnp.zeros((shared.shape[1] - rows, width), jnp.float32)], axis=0
     ).astype(jnp.bfloat16)
-    shared[me, 0:rows] = ready
-    outgoing = []
-    for d in range(1, n):
-        peer = lax.rem(me + d, n)
-        outgoing.append(
-            send(shared.at[me], shared.at[me], "seq", peer, send_b.at[d - 1], recv_b.at[d - 1])
-        )
+
+    def arrive(index):
+        held = shared[index].astype(jnp.float32)
+        for i in range(rows // steps):
+            out_ref[index * (rows // steps) + i] = held[i * steps : (i + 1) * steps]
+
+    copies += pair_gather(n, shared, sems[4:], arrive)
     for copy in copies:
-        copy.wait_send()
-    for copy in outgoing:
-        copy.wait_recv()
-    for j in range(n):
-        held = shared[j].astype(jnp.float32)
-        for i in range(rows // steps):
-            out_ref[j * (rows // steps) + i] = held[i * steps : (i + 1) * steps]
-    for copy in outgoing:
         copy.wait_send()
 
 
@@ -323,37 +413,39 @@
     idle_lane = lax.broadcasted_iota(jnp.int32, (steps, cols + LANES), 1)
     idle = jnp.where((idle_lane >= cols) & (idle_lane < cols + HALF_LANES), NEGATIVE, 0.0)
 
-    @pl.loop(0, requests)
-    def _(b):
-        used = is_used(b)
-
-        @pl.when(jnp.logical_not(used))
-        def _():
-            out_ref[b] = idle
-
-        @pl.when(used)
-        def _():
-            length = lengths_ref[b]
-            for p in range(local_pages):
-                page_copy(b, p).wait()
-            for u in range(steps):
-                spot = length + u - base
-
-                @pl.when((spot >= 0) & (spot < block_len))
-                def _():
-                    top = pl.multiple_of(spot // page_rows * page_rows, page_rows)
-                    hit = page_row == spot - top
-                    for kind in range(2):
-                        fresh = qkv_ref[b, u : u + 1, (kind + 1) * cols : (kind + 2) * cols]
-                        old = pages[b, kind, pl.ds(top, page_rows), :].astype(jnp.float32)
-                        pages[b, kind, pl.ds(top, page_rows), :] = jnp.where(
-                            hit, fresh, old
-                        ).astype(jnp.bfloat16)
-
+    together = 4
+
+    @pl.loop(0, requests // together)
+    def _(block):
+        for k in range(together):
+            b = block * together + k
+
+            @pl.when(is_used(b))
+            def _():
+                length = lengths_ref[b]
+                for p in range(local_pages):
+                    page_copy(b, p).wait()
+                for u in range(steps):
+                    spot = length + u - base
+
+                    @pl.when((spot >= 0) & (spot < block_len))
+                    def _():
+                        top = pl.multiple_of(spot // page_rows * page_rows, page_rows)
+                        hit = page_row == spot - top
+                        for kind in range(2):
+                            fresh = qkv_ref[b, u : u + 1, (kind + 1) * cols : (kind + 2) * cols]
+                            old = pages[b, kind, pl.ds(top, page_rows), :].astype(jnp.float32)
+                            pages[b, kind, pl.ds(top, page_rows), :] = jnp.where(
+                                hit, fresh, old
+                            ).astype(jnp.bfloat16)
+
+        batch = [block * together + k for k in range(together)]
+        all_scores = []
+        for b in batch:
             wide = jnp.concatenate(
                 [qkv_ref[b, t : t + 1, :cols] * own for t in range(steps)], axis=0
             ).astype(jnp.bfloat16)
-            scores = (
+            all_scores.append(
                 lax.dot_general(
                     wide,
                     pages[b, 0],
@@ -362,7 +454,9 @@
                 )
                 * scale
             )
-            reach = length + row_step
+        parts = []
+        for b, scores in zip(batch, all_scores):
+            reach = lengths_ref[b] + row_step
             live = (place <= reach) & ((place < SINKS) | (place > reach - WINDOW))
             scores = jnp.where(live, scores, NEGATIVE)
             peak = jnp.max(scores, axis=-1, keepdims=True)
@@ -370,17 +464,19 @@
             weight_sum = jnp.sum(weights, axis=-1, keepdims=True)
             coarse = weights.astype(jnp.bfloat16)
             fine = (weights - coarse.astype(jnp.float32)).astype(jnp.bfloat16)
-            both = jnp.dot(
-                jnp.concatenate([coarse, fine], axis=0),
-                pages[b, 1],
-                preferred_element_type=jnp.float32,
-            )
+            parts.append((peak, weight_sum, jnp.concatenate([coarse, fine], axis=0)))
+        for b, (peak, weight_sum, pieces) in zip(batch, parts):
+            both = jnp.dot(pieces, pages[b, 1], preferred_element_type=jnp.float32)
             weighted = both[: steps * heads] + both[steps * heads :]
+            used = is_used(b)
             for t in range(steps):
                 part = slice(t * heads, (t + 1) * heads)
-                out_ref[b, t : t + 1, :cols] = jnp.sum(weighted[part] * own, axis=0, keepdims=True)
-                out_ref[b, t : t + 1, cols:] = jnp.sum(
+                row = jnp.sum(weighted[part] * own, axis=0, keepdims=True)
+                stat = jnp.sum(
                     peak[part] * pick_peak + weight_sum[part] * pick_sum, axis=0, keepdims=True
+                )
+                out_ref[b, t : t + 1, :] = jnp.where(
+                    used, jnp.concatenate([row, stat], axis=1), idle[t : t + 1]
                 )
 
 
@@ -401,8 +497,10 @@
     flat,
     mid_landed,
     mid_all,
-    pair_out,
-    pair_landed,
+    near_out,
+    near_in,
+    far_out,
+    far_in,
     square_out,
     square_landed,
     acts,
@@ -410,36 +508,23 @@
     last,
     send_a,
     recv_a,
-    send_b,
-    recv_b,
-    send_c,
-    recv_c,
-    send_d,
-    recv_d,
-    send_e,
-    recv_e,
     send_s,
     recv_s,
-    send_f,
-    recv_f,
-    send_g,
-    recv_g,
-    send_h,
-    recv_h,
+    *sems,
 ):
     me = lax.axis_index("seq")
     rank = lax.axis_index("tp")
-    rows = chunks.shape[1]
+    tp_sems, seq_sems = sems[:8], sems[8:]
     steps = att_ref.shape[1]
     cols = wo_ref.shape[0]
     group = mid_all.shape[1]
     flat_rows = flat.shape[0]
     local_width = flat.shape[1]
     units = acts.shape[2]
+    rows = flat_rows // n
     per = rows // steps
     for j in range(n):
-        for i in range(per):
-            chunks[j, i * steps : (i + 1) * steps] = att_ref[j * per + i]
+        put_rows(chunks, j, jnp.concatenate([att_ref[j * per + i] for i in range(per)], axis=0))
     greet((("seq", n), ("tp", m)))
     copies = []
     for d in range(1, n):
@@ -449,7 +534,9 @@
         )
     for copy in copies:
         copy.wait_recv()
-    arrived = [chunks[me]] + [landed[d - 1] for d in range(1, n)]
+    arrived = [get_rows(chunks, me, cols + LANES)] + [
+        get_rows(landed, d - 1, cols + LANES) for d in range(1, n)
+    ]
     stats = [value[:, cols:] for value in arrived]
     lane = lax.broadcasted_iota(jnp.int32, (rows, LANES), 1)
     is_peak = lane < HALF_LANES
@@ -471,25 +558,16 @@
         attn = attn + value[:, :cols] * jnp.dot(
             share, spread, precision=lax.Precision.HIGHEST, preferred_element_type=jnp.float32
         )
-    shared[me, 0:rows] = attn.astype(jnp.bfloat16)
-    outgoing = []
-    for d in range(1, n):
-        peer = lax.rem(me + d, n)
-        outgoing.append(
-            send(shared.at[me], shared.at[me], "seq", peer, send_b.at[d - 1], recv_b.at[d - 1])
-        )
-    for copy in copies:
-        copy.wait_send()
-    for copy in outgoing:
-        copy.wait_recv()
     padded = shared.shape[1]
+    shared[me] = jnp.concatenate(
+        [attn, jnp.zeros((padded - rows, cols), jnp.float32)], axis=0
+    ).astype(jnp.bfloat16)
+    copies += pair_gather(n, shared, seq_sems[:4], lambda index: None)
     product = jnp.dot(
         shared[...].reshape(n * padded, cols), wo_ref[...], preferred_element_type=jnp.float32
     )
     for j in range(n):
         flat[j * rows : (j + 1) * rows, :] = product[j * padded : j * padded + rows]
-    for copy in outgoing:
-        copy.wait_send()
 
     def tp_scatter(target, send_sem, recv_sem):
         started = []
@@ -532,9 +610,9 @@
             copy.wait()
 
     own_rows = pl.ds(pl.multiple_of(rank * group, group), group)
-    mid_own = x_ref[own_rows, :] + tp_scatter(mid_landed, send_c, recv_c)
+    mid_own = x_ref[own_rows, :] + tp_scatter(mid_landed, *tp_sems[0:2])
     mid_all[rank] = mid_own
-    tp_gather(mid_all, send_d, recv_d)
+    tp_gather(mid_all, *tp_sems[2:4])
     mid = mid_all[...].reshape(flat_rows, local_width)
     mlp_in = (mid * gain_ref[...].astype(jnp.float32)).astype(jnp.bfloat16)
     square_out[...] = lax.dot_general(
@@ -553,27 +631,29 @@
 
     def pair(index):
         span = pl.ds(pl.multiple_of(index * units, units), units)
-        gate = jnp.dot(mlp_in, wg_ref[:, span], preferred_element_type=jnp.float32)
-        upward = jnp.dot(mlp_in, wu_ref[:, span], preferred_element_type=jnp.float32)
-        return gate, upward
-
-    pairs = []
-    for d in range(1, n):
-        peer = lax.rem(me + d, n)
-        gate, upward = pair(peer)
-        pair_out[d - 1, :, :units] = gate
-        pair_out[d - 1, :, units:] = upward
-        pairs.append(
-            send(
-                pair_out.at[d - 1],
-                pair_landed.at[d - 1],
-                "seq",
-                peer,
-                send_e.at[d - 1],
-                recv_e.at[d - 1],
-            )
+        return jnp.concatenate(
+            [
+                jnp.dot(mlp_in, wg_ref[:, span], preferred_element_type=jnp.float32),
+                jnp.dot(mlp_in, wu_ref[:, span], preferred_element_type=jnp.float32),
+            ],
+            axis=1,
         )
-    gate, upward = pair(me)
+
+    def put(ref, slot, value):
+        ref[slot] = value.astype(ref.dtype)
+
+    pair_total, pairs = pair_scatter(
+        n,
+        pair,
+        put,
+        lambda ref, slot: ref[slot].astype(jnp.float32),
+        near_out,
+        near_in,
+        far_out,
+        far_in,
+        seq_sems[4:8],
+    )
+    copies += pairs
     for copy in squares:
         copy.wait()
     square_sum = square_out[...]
@@ -587,35 +667,20 @@
         preferred_element_type=jnp.float32,
     )
     inv_mid = lax.rsqrt(column / D + EPSILON)
-    for d in range(1, n):
-        pairs[d - 1].wait_recv()
-        gate = gate + pair_landed[d - 1, :, :units]
-        upward = upward + pair_landed[d - 1, :, units:]
-    gate = gate * inv_mid
-    act = (gate / (1.0 + jnp.exp(-gate)) * (upward * inv_mid)).astype(jnp.bfloat16)
-    acts[0] = act
-    activated = []
-    for d in range(1, n):
-        peer = lax.rem(me + d, n)
-        activated.append(
-            send(acts.at[0], acts.at[d], "seq", peer, send_f.at[d - 1], recv_f.at[d - 1])
-        )
-
-    def down(slot, index):
+    gate = pair_total[:, :units] * inv_mid
+    act = gate / (1.0 + jnp.exp(-gate)) * (pair_total[:, units:] * inv_mid)
+    acts[me] = act.astype(jnp.bfloat16)
+    flat[...] = jnp.zeros_like(flat)
+
+    def down(index):
         span = pl.ds(pl.multiple_of(index * units, units), units)
-        return jnp.dot(acts[slot], wd_ref[span, :], preferred_element_type=jnp.float32)
-
-    product = down(0, me)
-    for copy in pairs:
+        flat[...] += jnp.dot(acts[index], wd_ref[span, :], preferred_element_type=jnp.float32)
+
+    copies += pair_gather(n, acts, seq_sems[8:12], down)
+    for copy in copies:
         copy.wait_send()
-    for d in range(1, n):
-        activated[d - 1].wait_recv()
-        product = product + down(d, lax.rem(me + n - d, n))
-    flat[...] = product
-    for copy in activated:
-        copy.wait_send()
-    last[rank] = (mid_own + tp_scatter(down_landed, send_g, recv_g)).astype(jnp.bfloat16)
-    tp_gather(last, send_h, recv_h)
+    last[rank] = (mid_own + tp_scatter(down_landed, *tp_sems[4:6])).astype(jnp.bfloat16)
+    tp_gather(last, *tp_sems[6:8])
     out_ref[...] = last[...]
 
 
@@ -675,18 +740,22 @@
     smem = pl.BlockSpec(memory_space=pltpu.SMEM)
     dma = pltpu.SemaphoreType.DMA
     wide = 3 * cols
+    half = n // 2
+    pair_sems = [dma((half,))] * 2 + [dma((half - 1,))] * 2
     qkv = pl.pallas_call(
         functools.partial(project_kernel, n),
         out_shape=jax.ShapeDtypeStruct((requests, steps, wide), f32),
         in_specs=[vmem] * 7,
         out_specs=vmem,
         scratch_shapes=[
-            pltpu.VMEM((flat_rows, wide + LANES), f32),
             pltpu.VMEM((n, rows, wide + LANES), f32),
-            pltpu.VMEM((n - 1, rows, wide + LANES), f32),
+            pltpu.VMEM((half, 8, packed_width(wide + LANES)), f32),
+            pltpu.VMEM((half, 8, packed_width(wide + LANES)), f32),
+            pltpu.VMEM((half - 1, 8, packed_width(wide + LANES)), f32),
+            pltpu.VMEM((half - 1, 8, packed_width(wide + LANES)), f32),
             pltpu.VMEM((n, padded, wide), bf16),
         ]
-        + [dma((n - 1,))] * 4,
+        + pair_sems * 2,
         compiler_params=pltpu.CompilerParams(
             collective_id=0, has_side_effects=True, vmem_limit_bytes=48 << 20
         ),
@@ -713,14 +782,16 @@
         in_specs=[vmem] * 7,
         out_specs=vmem,
         scratch_shapes=[
-            pltpu.VMEM((n, rows, cols + LANES), f32),
-            pltpu.VMEM((n - 1, rows, cols + LANES), f32),
+            pltpu.VMEM((n, 8, packed_width(cols + LANES)), f32),
+            pltpu.VMEM((n - 1, 8, packed_width(cols + LANES)), f32),
             pltpu.VMEM((n, padded, cols), bf16),
             pltpu.VMEM((flat_rows, local_width), f32),
             pltpu.VMEM((m - 1, group, local_width), f32),
             pltpu.VMEM((m, group, local_width), f32),
-            pltpu.VMEM((n - 1, flat_rows, 2 * units), f32),
-            pltpu.VMEM((n - 1, flat_rows, 2 * units), f32),
+            pltpu.VMEM((half, flat_rows, 2 * units), bf16),
+            pltpu.VMEM((half, flat_rows, 2 * units), bf16),
+            pltpu.VMEM((half - 1, flat_rows, 2 * units), bf16),
+            pltpu.VMEM((half - 1, flat_rows, 2 * units), bf16),
             pltpu.VMEM((8, flat_rows), f32),
             pltpu.VMEM((n - 1, 8, flat_rows), f32),
             pltpu.VMEM((n, flat_rows, units), bf16),
@@ -728,9 +799,8 @@
             pltpu.VMEM((m, group, local_width), bf16),
         ]
         + [dma((n - 1,))] * 4
-        + [dma((m - 1,))] * 4
-        + [dma((n - 1,))] * 6
-        + [dma((m - 1,))] * 4,
+        + [dma((m - 1,))] * 8
+        + pair_sems * 3,
         compiler_params=pltpu.CompilerParams(
             collective_id=1, has_side_effects=True, vmem_limit_bytes=48 << 20
         ),
@@ -742,9 +812,10 @@
 def fits(n, m):
     flat_rows = 96
     return (
-        n > 1
+        n % 2 == 0
+        and n > 2
         and m > 1
-        and flat_rows % (n * 4) == 0
+        and flat_rows == n * 12
         and flat_rows % (m * 8) == 0
         and D // m % LANES == 0
         and D // m // HEAD_DIM <= 8

time: 156 us -> 109 us (0.70); the launches traced: 153 us -> 109 us
  Pallas kernels: 148 us -> 103 us
    pallas_call x1, Pallas kernels: 80.5 us -> 58.9 us  [fused_body(): pl.pallas_call(functools.partial(finish_kernel, n, m), out_shape=jax.Shap...]
    pallas_call x1, Pallas kernels: 48.6 us -> 32.5 us  [fused_body(): pl.pallas_call(functools.partial(project_kernel, n), out_shape=jax.ShapeD...]
    pallas_call x1, Pallas kernels: 18.6 us -> 12 us  [fused_body(): pl.pallas_call(attend_kernel, out_shape=jax.ShapeDtypeStruct((requests, s...]
where the time goes in v2:
time: 109 us
  Pallas kernels  103 us (94%)
  local copies, waits for them, and re-layouts  3.4 us (3%)
  other arithmetic  1.27 us (1%)
    pallas_call x1, Pallas kernels, fused_body(): pl.pallas_call(functools.partial(finish_kernel, n, m), out_shape=jax.Shap...  58.9 us
    pallas_call x1, Pallas kernels, fused_body(): pl.pallas_call(functools.partial(project_kernel, n), out_shape=jax.ShapeD...  32.5 us
    pallas_call x1, Pallas kernels, fused_body(): pl.pallas_call(attend_kernel, out_shape=jax.ShapeDtypeStruct((requests, s...  12 us

profile of v2, /device:TPU:0, one launch (start us, length us, event | category | flops | bytes accessed | tf_op | source)
XLA Modules:
  0.0 108.9 jit_solution(7565822018262490667)
XLA Ops:
  0.6 0.7 add_convert_fusion
  1.4 0.1 convert_element_type.32
  1.5 0.3 multiply_sine_fusion
  1.7 0.1 tile.16
  1.8 0.0 copy-start.8
  1.8 0.0 copy-start.11
  1.8 0.0 copy-start.4
  1.8 0.0 copy-start.5
  1.8 0.0 copy-start.6
  1.9 0.4 tile.17.cos_ref
  2.2 0.1 tile.18
  2.3 0.4 tile.19.sin_ref
  2.6 0.0 copy-done.8
  2.7 0.0 copy-done.11
  2.8 0.2 copy-done.4
  2.9 0.2 copy-done.5
  3.1 0.2 copy-done.6
  3.3 0.0 copy-start.13
  3.3 0.0 copy-start.10
  3.3 0.0 copy-start.9
  3.3 0.0 copy-start.7
  3.3 32.5 %shard_map.158.qkv_ref = f32[24,4,2304]{2,1,0:T(4,128)S(1)} custom-call(bf16[96,384]{1,0:T(8,128)(2,1)S(1)} %reshape.155.x_ref, bf16[1,384]{1,0:T(2,128)(2,1)S(1)} %reshape.156.gain_ref, bf16[384,768]{1,0:T(8,128)(2,1)S(1)} %copy-done.4, bf16[384,768]{1,0:T(8,128)(2,1)S(1)} %copy-done.5, bf16[384,768]{1,0:T(8,128)(2,1)S(1)} %copy-done.6, ...), custom_call_target="tpu_custom_call" | custom-call | tf_op jit(solution)/shard_map/pallas_call | solution.py:745
  35.8 0.1 fusion
  35.9 0.0 copy-done.13
  35.9 0.0 copy-done.10
  35.9 0.1 multiply_reduce_fusion.1
  36.0 0.1 multiply_reduce_fusion
  36.1 0.1 copy.25
  36.1 0.0 copy-done.9
  36.1 0.1 copy.26
  36.2 0.0 copy-done.7
  36.2 0.0 copy-start.12
  36.2 0.0 copy-start
  36.2 0.0 copy-start.1
  36.3 0.0 copy-start.2
  36.3 0.0 copy-start.3
  36.3 12.0 %shard_map.159.att_ref = f32[24,4,896]{2,1,0:T(4,128)S(1)} custom-call(s32[24]{0:T(128)S(1)} %copy-done.7, s32[24,8]{1,0:T(8,128)S(1)} %broadcast_select_fusion.pages_ref, f32[24,4,2304]{2,1,0:T(4,128)S(1)} %shard_map.158.qkv_ref, bf16[2,208,32,768]{3,2,1,0:T(8,128)(2,1)} %kv_ref.1), custom_call_target="tpu_custom_call" | custom-call | tf_op jit(solution)/shard_map/pallas_call | solution.py:767
  48.4 0.0 copy-done.12
  48.4 0.0 copy-done
  48.4 0.0 copy-done.1
  48.4 0.0 copy-done.2
  48.4 0.0 copy-done.3
  48.4 58.9 %shard_map.160 = bf16[4,24,384]{2,1,0:T(8,128)(2,1)S(1)} custom-call(f32[24,4,896]{2,1,0:T(4,128)S(1)} %shard_map.159.att_ref, f32[96,384]{1,0:T(8,128)S(1)} %convert_element_type.33.x_ref, bf16[1,384]{1,0:T(2,128)(2,1)S(1)} %reshape.157.gain_ref, bf16[768,384]{1,0:T(8,128)(2,1)S(1)} %copy-done.3, bf16[384,2048]{1,0:T(8,128)(2,1)S(1)} %copy-done, ...), custom_call_target="tpu_custom_call" | custom-call | tf_op jit(solution)/shard_map/pallas_call | solution.py:779
  107.3 0.6 copy.33
  108.0 0.1 slice.7
  108.1 0.1 reshape.159
  108.2 0.8 copy.32
  (11 shorter events, 0.1 us)
Async XLA Ops:
  1.8 0.9 copy-start.8
  1.8 0.9 copy-start.11
  1.8 1.1 %copy-start.4 = (bf16[384,768]{1,0:T(8,128)(2,1)S(1)}, bf16[384,768]{1,0:T(8,128)(2,1)}, u32[]{:S(2)}) copy-start(bf16[384,768]{1,0:T(8,128)(2,1)} %wq_ref.1) | copy-start | bytes 1769476
  1.8 1.3 %copy-start.5 = (bf16[384,768]{1,0:T(8,128)(2,1)S(1)}, bf16[384,768]{1,0:T(8,128)(2,1)}, u32[]{:S(2)}) copy-start(bf16[384,768]{1,0:T(8,128)(2,1)} %wk_ref.1) | copy-start | bytes 1769476
  1.8 1.4 %copy-start.6 = (bf16[384,768]{1,0:T(8,128)(2,1)S(1)}, bf16[384,768]{1,0:T(8,128)(2,1)}, u32[]{:S(2)}) copy-start(bf16[384,768]{1,0:T(8,128)(2,1)} %wv_ref.1) | copy-start | bytes 1769476
  3.3 32.6 %copy-start.13 = (s32[24]{0:T(128)S(1)}, s32[24]{0:T(128)}, u32[]{:S(2)}) copy-start(s32[24]{0:T(128)} %param.27) | copy-start | bytes 292
  3.3 32.6 %copy-start.10 = (s32[2,16]{1,0:T(2,128)S(1)}, s32[2,16]{1,0:T(2,128)}, u32[]{:S(2)}) copy-start(s32[2,16]{1,0:T(2,128)} %param.28) | copy-start | bytes 388
  3.3 32.9 %copy-start.9 = (s32[24,8]{0,1:T(8,128)S(1)}, s32[24,8]{0,1:T(8,128)}, u32[]{:S(2)}) copy-start(s32[24,8]{0,1:T(8,128)} %param.29) | copy-start | bytes 2308
  3.3 32.9 %copy-start.7 = (s32[24]{0:T(128)S(1)}, s32[24]{0:T(128)}, u32[]{:S(2)}) copy-start(s32[24]{0:T(128)} %lengths_ref.1) | copy-start | bytes 292
  36.2 12.1 %copy-start.12 = (bf16[384]{0:T(512)(128)(2,1)S(1)}, bf16[384]{0:T(512)(128)(2,1)}, u32[]{:S(2)}) copy-start(bf16[384]{0:T(512)(128)(2,1)} %param.21) | copy-start | bytes 2308
  36.2 12.2 %copy-start = (bf16[384,2048]{1,0:T(8,128)(2,1)S(1)}, bf16[384,2048]{1,0:T(8,128)(2,1)}, u32[]{:S(2)}) copy-start(bf16[384,2048]{1,0:T(8,128)(2,1)} %wg_ref.1) | copy-start | bytes 4718596
  36.2 12.1 %copy-start.1 = (bf16[384,2048]{1,0:T(8,128)(2,1)S(1)}, bf16[384,2048]{1,0:T(8,128)(2,1)}, u32[]{:S(2)}) copy-start(bf16[384,2048]{1,0:T(8,128)(2,1)} %wu_ref.1) | copy-start | bytes 4718596
  36.3 12.1 %copy-start.2 = (bf16[2048,384]{1,0:T(8,128)(2,1)S(1)}, bf16[2048,384]{1,0:T(8,128)(2,1)}, u32[]{:S(2)}) copy-start(bf16[2048,384]{1,0:T(8,128)(2,1)} %wd_ref.1) | copy-start | bytes 4718596
  36.3 12.1 %copy-start.3 = (bf16[768,384]{1,0:T(8,128)(2,1)S(1)}, bf16[768,384]{1,0:T(8,128)(2,1)}, u32[]{:S(2)}) copy-start(bf16[768,384]{1,0:T(8,128)(2,1)} %wo_ref.1) | copy-start | bytes 1769476

commit v3 on v2

--- a/solution.py
+++ b/solution.py
@@ -295,6 +295,7 @@
     cos_ref,
     sin_ref,
     out_ref,
+    new_ref,
     partial,
     near_out,
     near_in,
@@ -347,17 +348,16 @@
         behind = pltpu.roll(vector, HEAD_DIM // 2, 1)
         return vector * cosine + jnp.where(early, -ahead, behind) * sine
 
-    ready = jnp.concatenate(
-        [
-            turn(projected[:, :cols]),
-            turn(projected[:, cols : 2 * cols]),
-            projected[:, 2 * cols :],
-        ],
-        axis=1,
-    )
-    shared[me] = jnp.concatenate(
-        [ready, jnp.zeros((shared.shape[1] - rows, width), jnp.float32)], axis=0
-    ).astype(jnp.bfloat16)
+    spare = shared.shape[1] - rows
+
+    def fill(value):
+        return jnp.concatenate(
+            [value, jnp.zeros((spare, value.shape[1]), jnp.float32)], axis=0
+        ).astype(jnp.bfloat16)
+
+    shared[me] = fill(turn(projected[:, :cols]))
+    new_ref[:, :cols] = fill(turn(projected[:, cols : 2 * cols]))
+    new_ref[:, cols:] = fill(projected[:, 2 * cols :])
 
     def arrive(index):
         held = shared[index].astype(jnp.float32)
@@ -369,11 +369,62 @@
         copy.wait_send()
 
 
+def head_masks(heads, cols):
+    head_row = lax.broadcasted_iota(jnp.int32, (heads, cols), 0) * HEAD_DIM
+    head_lane = lax.broadcasted_iota(jnp.int32, (heads, cols), 1)
+    own = jnp.where((head_lane >= head_row) & (head_lane < head_row + HEAD_DIM), 1.0, 0.0)
+    stat_lane = lax.broadcasted_iota(jnp.int32, (heads, LANES), 1)
+    stat_row = lax.broadcasted_iota(jnp.int32, (heads, LANES), 0)
+    pick_peak = jnp.where(stat_lane == stat_row, 1.0, 0.0)
+    pick_sum = jnp.where(stat_lane == stat_row + HALF_LANES, 1.0, 0.0)
+    return own, pick_peak, pick_sum
+
+
+def attend_new(queries, keys, values, steps, heads):
+    cols = queries[0].shape[1]
+    own, pick_peak, pick_sum = head_masks(heads, cols)
+    wide = jnp.concatenate(
+        [value[t : t + 1] * own for value in queries for t in range(steps)], axis=0
+    ).astype(jnp.bfloat16)
+    scores = lax.dot_general(
+        wide, keys, (((1,), (1,)), ((), ())), preferred_element_type=jnp.float32
+    ) * (1.0 / math.sqrt(HEAD_DIM))
+    query_row = lax.broadcasted_iota(jnp.int32, scores.shape, 0) // heads
+    key_row = lax.broadcasted_iota(jnp.int32, scores.shape, 1)
+    live = (key_row <= query_row) & (key_row // steps == query_row // steps)
+    scores = jnp.where(live, scores, NEGATIVE)
+    peak = jnp.max(scores, axis=-1, keepdims=True)
+    weights = jnp.where(live, jnp.exp(scores - peak), 0.0)
+    weight_sum = jnp.sum(weights, axis=-1, keepdims=True)
+    coarse = weights.astype(jnp.bfloat16)
+    fine = (weights - coarse.astype(jnp.float32)).astype(jnp.bfloat16)
+    weighted = jnp.dot(coarse, values, preferred_element_type=jnp.float32) + jnp.dot(
+        fine, values, preferred_element_type=jnp.float32
+    )
+    out = []
+    for index in range(len(queries) * steps):
+        part = slice(index * heads, (index + 1) * heads)
+        out.append(
+            jnp.concatenate(
+                [
+                    jnp.sum(weighted[part] * own, axis=0, keepdims=True),
+                    jnp.sum(
+                        peak[part] * pick_peak + weight_sum[part] * pick_sum,
+                        axis=0,
+                        keepdims=True,
+                    ),
+                ],
+                axis=1,
+            )
+        )
+    return jnp.concatenate(out, axis=0)
+
+
 def attend_kernel(
-    lengths_ref, pages_ref, qkv_ref, kv_ref, out_ref, pages, page_sem
+    lengths_ref, pages_ref, query_ref, kv_ref, out_ref, pages, page_sem
 ):
     seq_index = lax.axis_index("seq")
-    requests, steps = qkv_ref.shape[0], qkv_ref.shape[1]
+    requests, steps = query_ref.shape[0], query_ref.shape[1]
     cols = pages.shape[-1]
     block_len = pages.shape[2]
     local_pages = page_sem.shape[1]
@@ -391,7 +442,7 @@
 
     def is_used(b):
         length = lengths_ref[b]
-        return (base < length + steps) & ((base < SINKS) | (base + block_len > length - WINDOW))
+        return (base < length) & ((base < SINKS) | (base + block_len > length - WINDOW))
 
     @pl.loop(0, requests)
     def _(b):
@@ -400,16 +451,9 @@
             for p in range(local_pages):
                 page_copy(b, p).start()
 
-    head_row = lax.broadcasted_iota(jnp.int32, (heads, cols), 0) * HEAD_DIM
-    head_lane = lax.broadcasted_iota(jnp.int32, (heads, cols), 1)
-    own = jnp.where((head_lane >= head_row) & (head_lane < head_row + HEAD_DIM), 1.0, 0.0)
-    stat_lane = lax.broadcasted_iota(jnp.int32, (heads, LANES), 1)
-    stat_row = lax.broadcasted_iota(jnp.int32, (heads, LANES), 0)
-    pick_peak = jnp.where(stat_lane == stat_row, 1.0, 0.0)
-    pick_sum = jnp.where(stat_lane == stat_row + HALF_LANES, 1.0, 0.0)
+    own, pick_peak, pick_sum = head_masks(heads, cols)
     row_step = lax.broadcasted_iota(jnp.int32, (steps * heads, block_len), 0) // heads
     place = base + lax.broadcasted_iota(jnp.int32, (steps * heads, block_len), 1)
-    page_row = lax.broadcasted_iota(jnp.int32, (page_rows, cols), 0)
     idle_lane = lax.broadcasted_iota(jnp.int32, (steps, cols + LANES), 1)
     idle = jnp.where((idle_lane >= cols) & (idle_lane < cols + HALF_LANES), NEGATIVE, 0.0)
 
@@ -422,28 +466,14 @@
 
             @pl.when(is_used(b))
             def _():
-                length = lengths_ref[b]
                 for p in range(local_pages):
                     page_copy(b, p).wait()
-                for u in range(steps):
-                    spot = length + u - base
-
-                    @pl.when((spot >= 0) & (spot < block_len))
-                    def _():
-                        top = pl.multiple_of(spot // page_rows * page_rows, page_rows)
-                        hit = page_row == spot - top
-                        for kind in range(2):
-                            fresh = qkv_ref[b, u : u + 1, (kind + 1) * cols : (kind + 2) * cols]
-                            old = pages[b, kind, pl.ds(top, page_rows), :].astype(jnp.float32)
-                            pages[b, kind, pl.ds(top, page_rows), :] = jnp.where(
-                                hit, fresh, old
-                            ).astype(jnp.bfloat16)
 
         batch = [block * together + k for k in range(together)]
         all_scores = []
         for b in batch:
             wide = jnp.concatenate(
-                [qkv_ref[b, t : t + 1, :cols] * own for t in range(steps)], axis=0
+                [query_ref[b, t : t + 1, :] * own for t in range(steps)], axis=0
             ).astype(jnp.bfloat16)
             all_scores.append(
                 lax.dot_general(
@@ -456,8 +486,8 @@
             )
         parts = []
         for b, scores in zip(batch, all_scores):
-            reach = lengths_ref[b] + row_step
-            live = (place <= reach) & ((place < SINKS) | (place > reach - WINDOW))
+            length = lengths_ref[b]
+            live = (place < length) & ((place < SINKS) | (place > length + row_step - WINDOW))
             scores = jnp.where(live, scores, NEGATIVE)
             peak = jnp.max(scores, axis=-1, keepdims=True)
             weights = jnp.where(live, jnp.exp(scores - peak), 0.0)
@@ -490,7 +520,11 @@
     wg_ref,
     wu_ref,
     wd_ref,
+    query_ref,
+    fresh_ref,
     out_ref,
+    cache_ref,
+    fresh_all,
     chunks,
     landed,
     shared,
@@ -532,9 +566,18 @@
         copies.append(
             send(chunks.at[peer], landed.at[d - 1], "seq", peer, send_a.at[d - 1], recv_a.at[d - 1])
         )
+    heads = cols // HEAD_DIM
+    fresh = attend_new(
+        [query_ref[me * per + i] for i in range(per)],
+        fresh_ref[:, :cols],
+        fresh_ref[:, cols:],
+        steps,
+        heads,
+    )
+    fresh_all[me] = fresh_ref[...]
     for copy in copies:
         copy.wait_recv()
-    arrived = [get_rows(chunks, me, cols + LANES)] + [
+    arrived = [fresh, get_rows(chunks, me, cols + LANES)] + [
         get_rows(landed, d - 1, cols + LANES) for d in range(1, n)
     ]
     stats = [value[:, cols:] for value in arrived]
@@ -545,24 +588,43 @@
     factors = [jnp.exp(value - top) for value in peaks]
     sums = [pltpu.roll(value, HALF_LANES, 1) for value in stats]
     total_sum = functools.reduce(lambda a, b: a + b, [f * s for f, s in zip(factors, sums)])
-    heads = cols // HEAD_DIM
     inverse = 1.0 / jnp.where(lane < heads, total_sum, 1.0)
     spread_row = lax.broadcasted_iota(jnp.int32, (LANES, cols), 0) * HEAD_DIM
     spread_lane = lax.broadcasted_iota(jnp.int32, (LANES, cols), 1)
     spread = jnp.where(
         (spread_lane >= spread_row) & (spread_lane < spread_row + HEAD_DIM), 1.0, 0.0
-    )
+    ).astype(jnp.bfloat16)
     attn = jnp.zeros((rows, cols), jnp.float32)
-    for factor, value in zip(factors, arrived):
-        share = jnp.where(lane < heads, factor * inverse, 0.0)
-        attn = attn + value[:, :cols] * jnp.dot(
-            share, spread, precision=lax.Precision.HIGHEST, preferred_element_type=jnp.float32
-        )
+    blank = jnp.zeros((16 - rows, LANES), jnp.float32)
+    rest = jnp.concatenate(
+        [
+            jnp.concatenate([jnp.where(lane < heads, factor * inverse, 0.0), blank], axis=0)
+            for factor in factors
+        ],
+        axis=0,
+    )
+    shares = 0.0
+    for _ in range(3):
+        piece = rest.astype(jnp.bfloat16)
+        rest = rest - piece.astype(jnp.float32)
+        shares = shares + jnp.dot(piece, spread, preferred_element_type=jnp.float32)
+    for index, value in enumerate(arrived):
+        attn = attn + value[:, :cols] * shares[index * 16 : index * 16 + rows]
     padded = shared.shape[1]
     shared[me] = jnp.concatenate(
         [attn, jnp.zeros((padded - rows, cols), jnp.float32)], axis=0
     ).astype(jnp.bfloat16)
     copies += pair_gather(n, shared, seq_sems[:4], lambda index: None)
+    _, half, device = place_of(n)
+    partner = device(0, True)
+    near_send, near_recv, far_send, far_recv = seq_sems[12:16]
+
+    def pass_on(index, peer, send_sem, recv_sem):
+        return send(fresh_all.at[index], fresh_all.at[index], "seq", peer, send_sem, recv_sem)
+
+    cache_far = {}
+    for d in range(1, half):
+        cache_far[d] = pass_on(me, device(d, False), far_send.at[d - 1], far_recv.at[d - 1])
     product = jnp.dot(
         shared[...].reshape(n * padded, cols), wo_ref[...], preferred_element_type=jnp.float32
     )
@@ -679,9 +741,20 @@
     copies += pair_gather(n, acts, seq_sems[8:12], down)
     for copy in copies:
         copy.wait_send()
+    cache_near = [pass_on(me, partner, near_send.at[0], near_recv.at[0])]
+    for d in range(1, half):
+        cache_far[d].wait_recv()
+        cache_near.append(
+            pass_on(device(-d, False), partner, near_send.at[d], near_recv.at[d])
+        )
     last[rank] = (mid_own + tp_scatter(down_landed, *tp_sems[4:6])).astype(jnp.bfloat16)
     tp_gather(last, *tp_sems[6:8])
     out_ref[...] = last[...]
+    for copy in cache_near:
+        copy.wait()
+    for copy in cache_far.values():
+        copy.wait_send()
+    cache_ref[...] = fresh_all[...]
 
 
 def fused_body(
@@ -742,28 +815,27 @@
     wide = 3 * cols
     half = n // 2
     pair_sems = [dma((half,))] * 2 + [dma((half - 1,))] * 2
-    qkv = pl.pallas_call(
+    queries, fresh = pl.pallas_call(
         functools.partial(project_kernel, n),
-        out_shape=jax.ShapeDtypeStruct((requests, steps, wide), f32),
+        out_shape=(
+            jax.ShapeDtypeStruct((requests, steps, cols), f32),
+            jax.ShapeDtypeStruct((padded, 2 * cols), bf16),
+        ),
         in_specs=[vmem] * 7,
-        out_specs=vmem,
+        out_specs=(vmem, vmem),
         scratch_shapes=[
             pltpu.VMEM((n, rows, wide + LANES), f32),
             pltpu.VMEM((half, 8, packed_width(wide + LANES)), f32),
             pltpu.VMEM((half, 8, packed_width(wide + LANES)), f32),
             pltpu.VMEM((half - 1, 8, packed_width(wide + LANES)), f32),
             pltpu.VMEM((half - 1, 8, packed_width(wide + LANES)), f32),
-            pltpu.VMEM((n, padded, wide), bf16),
+            pltpu.VMEM((n, padded, cols), bf16),
         ]
         + pair_sems * 2,
         compiler_params=pltpu.CompilerParams(
             collective_id=0, has_side_effects=True, vmem_limit_bytes=48 << 20
         ),
     )(x, attn_gain.reshape(1, -1), w_query, w_key, w_value, cosine, sine)
-    new_cache = jnp.transpose(
-        qkv[:, :, cols:].astype(bf16).reshape(requests, steps, 2, cols), (2, 1, 0, 3)
-    )
-
     attended = pl.pallas_call(
         attend_kernel,
         out_shape=jax.ShapeDtypeStruct((requests, steps, cols + LANES), f32),
@@ -774,14 +846,18 @@
             dma((requests, local_pages)),
         ],
         compiler_params=pltpu.CompilerParams(vmem_limit_bytes=48 << 20),
-    )(lengths, physical, qkv, kv_pages)
-
-    result = pl.pallas_call(
+    )(lengths, physical, queries, kv_pages)
+
+    result, caches = pl.pallas_call(
         functools.partial(finish_kernel, n, m),
-        out_shape=jax.ShapeDtypeStruct((m, group, local_width), bf16),
-        in_specs=[vmem] * 7,
-        out_specs=vmem,
+        out_shape=(
+            jax.ShapeDtypeStruct((m, group, local_width), bf16),
+            jax.ShapeDtypeStruct((n, padded, 2 * cols), bf16),
+        ),
+        in_specs=[vmem] * 9,
+        out_specs=(vmem, vmem),
         scratch_shapes=[
+            pltpu.VMEM((n, padded, 2 * cols), bf16),
             pltpu.VMEM((n, 8, packed_width(cols + LANES)), f32),
             pltpu.VMEM((n - 1, 8, packed_width(cols + LANES)), f32),
             pltpu.VMEM((n, padded, cols), bf16),
@@ -800,11 +876,24 @@
         ]
         + [dma((n - 1,))] * 4
         + [dma((m - 1,))] * 8
-        + pair_sems * 3,
+        + pair_sems * 4,
         compiler_params=pltpu.CompilerParams(
             collective_id=1, has_side_effects=True, vmem_limit_bytes=48 << 20
         ),
-    )(attended, x.astype(f32), mlp_gain.reshape(1, -1), w_out, w_gate, w_up, w_down)
+    )(
+        attended,
+        x.astype(f32),
+        mlp_gain.reshape(1, -1),
+        w_out,
+        w_gate,
+        w_up,
+        w_down,
+        queries,
+        fresh,
+    )
+    new_cache = jnp.transpose(
+        caches[:, :rows].reshape(requests, steps, 2, cols), (2, 1, 0, 3)
+    )
     hidden_out = jnp.transpose(result.reshape(requests, steps, local_width), (1, 0, 2))
     return (hidden_out, new_cache)
 

time: 109 us -> 109 us (level)
  Pallas kernels: 103 us -> 101 us
  local copies, waits for them, and re-layouts: 3.4 us -> 4.77 us
    another operation x2, local copies, waits for them, and re-layouts: 0.42 us -> 2.41 us  [fused_body(): jnp.tile(jnp.sin(angles), (1, cols // halfway)).reshape(n, rows, cols)]
    pallas_call x2, Pallas kernels: 91.3 us -> 89.8 us  [the longest x1 59.6 us: fused_body(): pl.pallas_call(functools.partial(finish_kernel, n, m), out_shape=(jax.Sha...]
where the time goes in v3:
time: 109 us; the launch traced here: 108 us
  Pallas kernels  101 us (93%)
  local copies, waits for them, and re-layouts  4.77 us (4%)
  other arithmetic  1.27 us (1%)
    pallas_call x1, Pallas kernels, fused_body(): pl.pallas_call(functools.partial(finish_kernel, n, m), out_shape=(jax.Sha...  59.6 us
    pallas_call x1, Pallas kernels, fused_body(): pl.pallas_call(functools.partial(project_kernel, n), out_shape=(jax.Shape...  30.2 us
    pallas_call x1, Pallas kernels, fused_body(): pl.pallas_call(attend_kernel, out_shape=jax.ShapeDtypeStruct((requests, s...  11.7 us
    another operation x2, local copies, waits for them, and re-layouts, fused_body(): jnp.tile(jnp.sin(angles), (1, cols // halfway)).reshape(n, rows, cols)  2.41 us

profile of v3, /device:TPU:0, one launch (start us, length us, event | category | flops | bytes accessed | tf_op | source)
XLA Modules:
  0.0 108.4 jit_solution(2525167828147954246)
XLA Ops:
  0.6 0.7 add_convert_fusion
  1.4 0.1 convert_element_type.31
  1.5 0.3 multiply_sine_fusion
  1.7 0.1 tile.16
  1.8 0.0 copy-start.7
  1.8 0.0 copy-start.10
  1.8 0.0 copy-start.2
  1.8 0.0 copy-start.3
  1.8 0.0 copy-start.4
  1.9 0.4 tile.17.cos_ref
  2.2 0.9 tile.18
  3.1 1.5 %tile.19.sin_ref = f32[8,12,768]{2,1,0:T(8,128)S(1)} reshape(f32[96,16,48]{2,1,0:T(8,128)} %tile.18) | data formatting | bytes 589824 | tf_op jit(solution)/shard_map/tile | solution.py:810
  4.6 0.0 copy-start.12
  4.6 0.0 copy-start.9
  4.7 0.0 copy-start.8
  4.7 0.0 copy-start.6
  4.7 0.0 copy-done.7
  4.7 0.0 copy-done.10
  4.8 0.0 copy-done.2
  4.8 0.0 copy-done.3
  4.8 0.0 copy-done.4
  4.8 30.2 %shard_map.158 = (f32[24,4,768]{2,1,0:T(4,128)S(1)}, bf16[16,1536]{1,0:T(8,128)(2,1)S(1)}) custom-call(bf16[96,384]{1,0:T(8,128)(2,1)S(1)} %reshape.155.x_ref, bf16[1,384]{1,0:T(2,128)(2,1)S(1)} %reshape.156.gain_ref, bf16[384,768]{1,0:T(8,128)(2,1)S(1)} %copy-done.2, bf16[384,768]{1,0:T(8,128)(2,1)S(1)} %copy-done.3, bf16[384,768]{1,0:T(8,128)(2,1)S(1)} %copy-done.4, ...), custom_call_target="tpu_custom_call" | custom-call | tf_op jit(solution)/shard_map/pallas_call | solution.py:818
  35.0 0.1 fusion
  35.1 0.0 copy-done.12
  35.1 0.0 copy-done.9
  35.1 0.1 multiply_reduce_fusion.1
  35.2 0.1 multiply_reduce_fusion
  35.3 0.1 copy.25
  35.4 0.0 copy-done.8
  35.4 0.1 copy.26
  35.5 0.0 copy-done.6
  35.5 0.0 copy-start.11
  35.5 0.0 copy-start
  35.5 0.0 copy-start.1
  35.5 0.0 copy-start.5
  35.5 11.7 %shard_map.159.att_ref = f32[24,4,896]{2,1,0:T(4,128)S(1)} custom-call(s32[24]{0:T(128)S(1)} %copy-done.6, s32[24,8]{1,0:T(8,128)S(1)} %broadcast_select_fusion.pages_ref, f32[24,4,768]{2,1,0:T(4,128)S(1)} %get-tuple-element.6.query_ref, bf16[2,208,32,768]{3,2,1,0:T(8,128)(2,1)} %kv_ref.1), custom_call_target="tpu_custom_call" | custom-call | tf_op jit(solution)/shard_map/pallas_call | solution.py:839
  47.2 0.0 copy-done.11
  47.2 0.0 copy-done
  47.2 0.0 copy-done.1
  47.2 0.0 copy-done.5
  47.2 59.6 %shard_map.160 = (bf16[4,24,384]{2,1,0:T(8,128)(2,1)S(1)}, bf16[8,16,1536]{2,1,0:T(8,128)(2,1)S(1)}) custom-call(f32[24,4,896]{2,1,0:T(4,128)S(1)} %shard_map.159.att_ref, f32[96,384]{1,0:T(8,128)S(1)} %convert_element_type.32.x_ref, bf16[1,384]{1,0:T(2,128)(2,1)S(1)} %reshape.157.gain_ref, bf16[768,384]{1,0:T(8,128)(2,1)S(1)} %copy-done.5, ...), custom_call_target="tpu_custom_call" | custom-call | tf_op jit(solution)/shard_map/pallas_call | solution.py:851
  106.8 0.1 reshape.159
  106.9 0.8 copy.29
  107.7 0.6 copy.31
  (11 shorter events, 0.1 us)
Async XLA Ops:
  1.8 2.9 %copy-start.7 = (bf16[4,24,384]{2,1,0:T(8,128)(2,1)S(1)}, bf16[4,24,384]{2,1,0:T(8,128)(2,1)}, u32[]{:S(2)}) copy-start(bf16[4,24,384]{2,1,0:T(8,128)(2,1)} %param.15) | copy-start | bytes 221188
  1.8 2.9 %copy-start.10 = (bf16[384]{0:T(512)(128)(2,1)S(1)}, bf16[384]{0:T(512)(128)(2,1)}, u32[]{:S(2)}) copy-start(bf16[384]{0:T(512)(128)(2,1)} %param.16) | copy-start | bytes 2308
  1.8 3.0 %copy-start.2 = (bf16[384,768]{1,0:T(8,128)(2,1)S(1)}, bf16[384,768]{1,0:T(8,128)(2,1)}, u32[]{:S(2)}) copy-start(bf16[384,768]{1,0:T(8,128)(2,1)} %wq_ref.1) | copy-start | bytes 1769476
  1.8 3.0 %copy-start.3 = (bf16[384,768]{1,0:T(8,128)(2,1)S(1)}, bf16[384,768]{1,0:T(8,128)(2,1)}, u32[]{:S(2)}) copy-start(bf16[384,768]{1,0:T(8,128)(2,1)} %wk_ref.1) | copy-start | bytes 1769476
  1.8 3.0 %copy-start.4 = (bf16[384,768]{1,0:T(8,128)(2,1)S(1)}, bf16[384,768]{1,0:T(8,128)(2,1)}, u32[]{:S(2)}) copy-start(bf16[384,768]{1,0:T(8,128)(2,1)} %wv_ref.1) | copy-start | bytes 1769476
  4.6 30.5 %copy-start.12 = (s32[24]{0:T(128)S(1)}, s32[24]{0:T(128)}, u32[]{:S(2)}) copy-start(s32[24]{0:T(128)} %param.27) | copy-start | bytes 292
  4.6 30.5 %copy-start.9 = (s32[2,16]{1,0:T(2,128)S(1)}, s32[2,16]{1,0:T(2,128)}, u32[]{:S(2)}) copy-start(s32[2,16]{1,0:T(2,128)} %param.28) | copy-start | bytes 388
  4.7 30.7 %copy-start.8 = (s32[24,8]{0,1:T(8,128)S(1)}, s32[24,8]{0,1:T(8,128)}, u32[]{:S(2)}) copy-start(s32[24,8]{0,1:T(8,128)} %param.29) | copy-start | bytes 2308
  4.7 30.8 %copy-start.6 = (s32[24]{0:T(128)S(1)}, s32[24]{0:T(128)}, u32[]{:S(2)}) copy-start(s32[24]{0:T(128)} %lengths_ref.1) | copy-start | bytes 292
  35.5 11.7 %copy-start.11 = (bf16[384]{0:T(512)(128)(2,1)S(1)}, bf16[384]{0:T(512)(128)(2,1)}, u32[]{:S(2)}) copy-start(bf16[384]{0:T(512)(128)(2,1)} %param.21) | copy-start | bytes 2308
  35.5 11.7 %copy-start = (bf16[384,2048]{1,0:T(8,128)(2,1)S(1)}, bf16[384,2048]{1,0:T(8,128)(2,1)}, u32[]{:S(2)}) copy-start(bf16[384,2048]{1,0:T(8,128)(2,1)} %wg_ref.1) | copy-start | bytes 4718596
  35.5 11.7 %copy-start.1 = (bf16[384,2048]{1,0:T(8,128)(2,1)S(1)}, bf16[384,2048]{1,0:T(8,128)(2,1)}, u32[]{:S(2)}) copy-start(bf16[384,2048]{1,0:T(8,128)(2,1)} %wu_ref.1) | copy-start | bytes 4718596
  35.5 11.7 %copy-start.5 = (bf16[768,384]{1,0:T(8,128)(2,1)S(1)}, bf16[768,384]{1,0:T(8,128)(2,1)}, u32[]{:S(2)}) copy-start(bf16[768,384]{1,0:T(8,128)(2,1)} %wo_ref.1) | copy-start | bytes 1769476

commit v4 on v3

--- a/solution.py
+++ b/solution.py
@@ -179,7 +179,7 @@
                 device_id_type=MESH_ID,
             )
             total += 1
-    pl.semaphore_wait(barrier, total)
+    return lambda: pl.semaphore_wait(barrier, total)
 
 
 def send(source, target, axis, peer, send_sem, recv_sem):
@@ -309,6 +309,7 @@
     width = 3 * cols
     steps = out_ref.shape[1]
     rows = cos_ref.shape[1]
+    all_here = greet((("seq", n),))
     x = x_ref[...].astype(jnp.float32)
     normed = (x * gain_ref[...].astype(jnp.float32)).astype(jnp.bfloat16)
     squares = jnp.sum(x * x, axis=-1, keepdims=True)
@@ -324,7 +325,7 @@
             (index + 1) * cols,
         )
     store(jnp.broadcast_to(squares, (x.shape[0], LANES)), width, width + LANES)
-    greet((("seq", n),))
+    all_here()
     total, copies = pair_scatter(
         n,
         lambda index: partial[index],
@@ -340,8 +341,8 @@
     projected = total[:, :width] * inv_rms
     lane = lax.broadcasted_iota(jnp.int32, (rows, cols), 1)
     early = lax.rem(lane, HEAD_DIM) < HEAD_DIM // 2
-    cosine = cos_ref[me]
-    sine = sin_ref[me]
+    cosine = jnp.concatenate([cos_ref[me]] * (cols // HEAD_DIM), axis=1)
+    sine = jnp.concatenate([sin_ref[me]] * (cols // HEAD_DIM), axis=1)
 
     def turn(vector):
         ahead = pltpu.roll(vector, cols - HEAD_DIM // 2, 1)
@@ -557,9 +558,10 @@
     units = acts.shape[2]
     rows = flat_rows // n
     per = rows // steps
+    all_here = greet((("seq", n), ("tp", m)))
     for j in range(n):
         put_rows(chunks, j, jnp.concatenate([att_ref[j * per + i] for i in range(per)], axis=0))
-    greet((("seq", n), ("tp", m)))
+    all_here()
     copies = []
     for d in range(1, n):
         peer = lax.rem(me + d, n)
@@ -806,8 +808,8 @@
     frequency = ROPE_BASE ** (-(jnp.arange(halfway, dtype=f32) * 2.0 / HEAD_DIM))
     where_now = (lengths[:, None] + jnp.arange(steps, dtype=jnp.int32)[None, :]).reshape(-1)
     angles = where_now[:, None].astype(f32) * frequency
-    cosine = jnp.tile(jnp.cos(angles), (1, cols // halfway)).reshape(n, rows, cols)
-    sine = jnp.tile(jnp.sin(angles), (1, cols // halfway)).reshape(n, rows, cols)
+    cosine = jnp.tile(jnp.cos(angles), (1, 2)).reshape(n, rows, HEAD_DIM)
+    sine = jnp.tile(jnp.sin(angles), (1, 2)).reshape(n, rows, HEAD_DIM)
 
     vmem = pl.BlockSpec(memory_space=pltpu.VMEM)
     smem = pl.BlockSpec(memory_space=pltpu.SMEM)

time: 109 us -> 112 us (1.028)
  local copies, waits for them, and re-layouts: 4.77 us -> 6.19 us
  other arithmetic: 1.27 us -> 2.68 us
    another operation x4, local copies, waits for them, and re-layouts: 2.83 us -> 0.3 us  [the longest x2 0.15 us: fused_body(): sine = jnp.tile(jnp.sin(angles), (1, 2)).reshape(n, rows, HEAD_DIM)]
    unnamed x28 -> x16, local copies, waits for them, and re-layouts: 0.92 us -> 2.62 us
where the time goes in v4:
time: 112 us
  Pallas kernels  102 us (91%)
  local copies, waits for them, and re-layouts  6.19 us (6%)
  other arithmetic  2.68 us (2%)
    pallas_call x1, Pallas kernels, fused_body(): pl.pallas_call(functools.partial(finish_kernel, n, m), out_shape=(jax.Sha...  60.3 us
    pallas_call x1, Pallas kernels, fused_body(): pl.pallas_call(functools.partial(project_kernel, n), out_shape=(jax.Shape...  29.8 us
    pallas_call x1, Pallas kernels, fused_body(): pl.pallas_call(attend_kernel, out_shape=jax.ShapeDtypeStruct((requests, s...  12 us
    unnamed x16, local copies, waits for them, and re-layouts  2.62 us

profile of v4, /device:TPU:0, one launch (start us, length us, event | category | flops | bytes accessed | tf_op | source)
XLA Modules:
  0.0 111.8 jit_solution(11496588900478255691)
XLA Ops:
  0.6 0.0 copy-start.3
  0.6 0.0 copy-start.2
  0.7 0.7 compare_convert_fusion
  1.4 0.7 reshape.156.gain_ref
  2.1 0.7 reshape.157.gain_ref
  2.8 0.1 fusion
  2.9 0.8 multiply_reduce_fusion.1
  3.6 0.1 multiply_reduce_fusion
  3.7 0.1 copy.25
  3.8 0.8 copy.26
  4.6 0.7 add_convert_fusion
  5.3 0.1 convert_element_type.31
  5.4 0.9 copy.27
  6.3 0.0 copy-start.6
  6.4 0.2 multiply_sine_fusion
  6.7 0.1 tile.19.sin_ref
  6.8 0.1 tile.17.cos_ref
  6.9 0.0 copy-done.3
  6.9 0.0 copy-done.2
  7.0 0.0 copy-start.4
  7.0 1.1 copy-done.4
  8.0 29.8 %shard_map.158 = (f32[24,4,768]{2,1,0:T(4,128)S(1)}, bf16[16,1536]{1,0:T(8,128)(2,1)S(1)}) custom-call(bf16[96,384]{1,0:T(8,128)(2,1)S(1)} %reshape.155.x_ref, bf16[1,384]{1,0:T(2,128)(2,1)S(1)} %reshape.156.gain_ref, bf16[384,768]{1,0:T(8,128)(2,1)S(1)} %copy-done.2, bf16[384,768]{1,0:T(8,128)(2,1)S(1)} %copy-done.3, bf16[384,768]{1,0:T(8,128)(2,1)S(1)} %copy-done.4, ...), custom_call_target="tpu_custom_call" | custom-call | tf_op jit(solution)/shard_map/pallas_call | solution.py:820
  37.8 0.0 copy-done.6
  37.8 0.0 copy-start
  37.8 0.0 copy-start.1
  37.9 0.0 copy-start.5
  37.9 12.0 %shard_map.159.att_ref = f32[24,4,896]{2,1,0:T(4,128)S(1)} custom-call(s32[24]{0:T(128)S(1)} %copy-done.6, s32[24,8]{1,0:T(8,128)S(1)} %broadcast_select_fusion.pages_ref, f32[24,4,768]{2,1,0:T(4,128)S(1)} %get-tuple-element.6.query_ref, bf16[2,208,32,768]{3,2,1,0:T(8,128)(2,1)} %kv_ref.1), custom_call_target="tpu_custom_call" | custom-call | tf_op jit(solution)/shard_map/pallas_call | solution.py:841
  49.9 0.0 copy-done
  49.9 0.0 copy-done.1
  49.9 0.0 copy-done.5
  49.9 60.3 %shard_map.160 = (bf16[4,24,384]{2,1,0:T(8,128)(2,1)S(1)}, bf16[8,16,1536]{2,1,0:T(8,128)(2,1)S(1)}) custom-call(f32[24,4,896]{2,1,0:T(4,128)S(1)} %shard_map.159.att_ref, f32[96,384]{1,0:T(8,128)S(1)} %convert_element_type.32.x_ref, bf16[1,384]{1,0:T(2,128)(2,1)S(1)} %reshape.157.gain_ref, bf16[768,384]{1,0:T(8,128)(2,1)S(1)} %copy-done.5, ...), custom_call_target="tpu_custom_call" | custom-call | tf_op jit(solution)/shard_map/pallas_call | solution.py:853
  110.2 0.6 copy.31
  110.9 0.1 reshape.159
  111.0 0.8 copy.29
  (9 shorter events, 0.2 us)
Async XLA Ops:
  0.6 6.3 %copy-start.3 = (bf16[384,768]{1,0:T(8,128)(2,1)S(1)}, bf16[384,768]{1,0:T(8,128)(2,1)}, u32[]{:S(2)}) copy-start(bf16[384,768]{1,0:T(8,128)(2,1)} %wk_ref.1) | copy-start | bytes 1769476
  0.6 6.3 %copy-start.2 = (bf16[384,768]{1,0:T(8,128)(2,1)S(1)}, bf16[384,768]{1,0:T(8,128)(2,1)}, u32[]{:S(2)}) copy-start(bf16[384,768]{1,0:T(8,128)(2,1)} %wq_ref.1) | copy-start | bytes 1769476
  6.3 31.5 %copy-start.6 = (s32[24]{0:T(128)S(1)}, s32[24]{0:T(128)}, u32[]{:S(2)}) copy-start(s32[24]{0:T(128)} %lengths_ref.1) | copy-start | bytes 292
  7.0 1.1 copy-start.4
  37.8 12.1 %copy-start = (bf16[384,2048]{1,0:T(8,128)(2,1)S(1)}, bf16[384,2048]{1,0:T(8,128)(2,1)}, u32[]{:S(2)}) copy-start(bf16[384,2048]{1,0:T(8,128)(2,1)} %wg_ref.1) | copy-start | bytes 4718596
  37.8 12.1 %copy-start.1 = (bf16[384,2048]{1,0:T(8,128)(2,1)S(1)}, bf16[384,2048]{1,0:T(8,128)(2,1)}, u32[]{:S(2)}) copy-start(bf16[384,2048]{1,0:T(8,128)(2,1)} %wu_ref.1) | copy-start | bytes 4718596
  37.9 12.1 %copy-start.5 = (bf16[768,384]{1,0:T(8,128)(2,1)S(1)}, bf16[768,384]{1,0:T(8,128)(2,1)}, u32[]{:S(2)}) copy-start(bf16[768,384]{1,0:T(8,128)(2,1)} %wo_ref.1) | copy-start | bytes 1769476
